TPU v7x, 32 devices: a whole 2x2x4 slice. The times are simulated.
32 devices in a mesh: row: 4 (over y, core), col: 8 (over z, x).
Axes of the slice: x: 2, y: 2, z: 4, core: 2. Of those that a mesh axis runs over, the one named last changes fastest.
Arguments:
- start_block: float32 [64, 65536], P(None, ('row', 'col')), may hold values from -6 to 6
- struct_blocks: bfloat16 [3, 512, 4, 128, 128], P(None, ('row', 'col'))
- block_ids: int32 [512, 4], P(('row', 'col')), may hold values from 0 to 17, as said below
- rim_rows: int32 [4096], P(('row', 'col')), may hold values from 0 to 2047, as said below
- wet_slots: int32 [32768], P(('row', 'col')), may hold values from 0 to 2047, as said below
- wet_counts: int32 [32], P(('row', 'col')), may hold values from 341 to 1024
- added_mass: bfloat16 [1024, 32768], P('col', 'row'), may hold values from -0.03125 to 0.03125
- coupling_rates: float32 [2], replicated, may hold values from 0.5 to 1.5
Outputs:
- lanczos_block: float32 [64, 65536], P(None, ('row', 'col'))
- coefficients: float32 [6, 3, 64, 64], replicated
Inputs may be any that keep to these rules, and one draw needn't show every extreme that they name: `block_ids`: each block row's first entry is its own local block row; the first local block row names 2048//128 (rim of the shard before) as its second entry and the last names 17; entries may repeat. `rim_rows`: local indices into a shard's 2048 degrees of freedom, distinct within one shard. `wet_slots`: local indices into a shard's 2048 degrees of freedom, distinct within one shard.
All inputs are finite; a program needn't handle non-finite values.
Results may differ from a plain program's by a relative error of at most 0.023.
Values may be sent and summed in bfloat16 or wider, within the bound.
No kernel may reach another device: no remote copies, remote signals or barrier semaphores. Data moves between devices by JAX's collectives and lax.ppermute only.
A program may use at most 128 MiB of HBM per device.

v0:
```python
import jax
import jax.numpy as jnp
from jax import lax
from jax.sharding import PartitionSpec as P

STEPS = 6


def from_behind(shard, axis, by):
    peers = lax.axis_size(axis)
    pairs = [(i, i + by) for i in range(peers) if 0 <= i + by < peers]
    return lax.ppermute(shard, axis, pairs)


def contract_rows(left, right):
    return lax.dot_general(left, right, (((1,), (1,)), ((), ())), precision=lax.Precision.HIGHEST)


def local(
    start_block,
    struct_blocks,
    block_ids,
    rim_rows,
    wet_slots,
    wet_counts,
    added_mass,
    coupling_rates,
):
    vectors = start_block.shape[0]
    shard_rows = start_block.shape[1]
    block_size = struct_blocks.shape[3]
    block_count = shard_rows // block_size
    total_rows = shard_rows * lax.axis_size("row") * lax.axis_size("col")
    live_slots = jnp.arange(wet_slots.shape[0]) < wet_counts[0]
    current = start_block
    previous = jnp.zeros_like(start_block)
    coefficients = []
    for number in range(STEPS):
        block_bf = current.astype(jnp.bfloat16)
        rim_values = block_bf[:, rim_rows]
        below_rim = from_behind(rim_values, ("row", "col"), 1)
        above_rim = from_behind(rim_values, ("row", "col"), -1)
        slot_values = jnp.where(
            live_slots[None, :], block_bf[:, wet_slots], jnp.zeros((), block_bf.dtype)
        )
        partial_sum = lax.dot_general(
            added_mass,
            lax.all_gather(slot_values, "col", axis=1, tiled=True),
            (((1,), (1,)), ((), ())),
            preferred_element_type=jnp.float32,
        )
        pressure = lax.psum_scatter(
            partial_sum.astype(jnp.bfloat16), "row", scatter_dimension=0, tiled=True
        ).astype(jnp.float32)
        extended = jnp.concatenate([block_bf, below_rim, above_rim], 1).reshape(
            vectors, block_count + 2, block_size
        )
        picked = extended[:, block_ids]
        products = jnp.einsum(
            "vikb,mikab->mvia", picked, struct_blocks, preferred_element_type=jnp.float32
        ).reshape(3, vectors, shard_rows)
        wet_force = (
            jnp.zeros((vectors, shard_rows), jnp.float32)
            .at[:, wet_slots[: pressure.shape[0]]]
            .add(pressure.T)
        )
        applied = (
            products[0]
            + coupling_rates[0] * products[1]
            - coupling_rates[1] * (products[2] + wet_force)
        )
        projected = lax.psum(
            (contract_rows(applied, current), contract_rows(applied, previous)), ("row", "col")
        )
        coef_self = projected[0] / total_rows
        coef_prev = projected[1] / total_rows
        residual = (
            applied
            - jnp.dot(coef_self, current, precision=lax.Precision.HIGHEST)
            - jnp.dot(coef_prev, previous, precision=lax.Precision.HIGHEST)
        )
        gram_matrix = lax.psum(contract_rows(residual, residual), ("row", "col")) / total_rows
        factor = jnp.linalg.cholesky(gram_matrix)
        following = lax.linalg.triangular_solve(factor, residual, left_side=True, lower=True)
        coefficients.append(jnp.stack([coef_self, coef_prev, factor]))
        previous = current
        current = following
    return (current, jnp.stack(coefficients))


def solution(mesh):
    return jax.shard_map(
        local,
        mesh=mesh,
        in_specs=(
            P(None, ("row", "col")),
            P(None, ("row", "col"), None, None, None),
            P(("row", "col"), None),
            P(("row", "col")),
            P(("row", "col")),
            P(("row", "col")),
            P("col", "row"),
            P(),
        ),
        out_specs=(P(None, ("row", "col")), P()),
        check_vma=False,
    )
```

profile of v0, /device:TPU:0, one launch (start us, length us, event | category | flops | bytes accessed | tf_op | source)
XLA Modules:
  0.0 1133.5 jit_solution(12181711351886117716)
XLA Ops:
  10.7 3.2 gather_fusion.2
  15.6 4.8 collective-permute-start
  30.5 6.0 fusion.12
  36.5 30.6 %all-gather.7.cloned.1.call-done = bf16[64,8192]{0,1:T(8,128)(2,1)} async-done(((bf16[64,1024]{0,1:T(8,128)(2,1)}), bf16[64,8192]{0,1:T(8,128)(2,1)}) %all-gather.7.cloned.1.call-update) | async-done | bytes 1048592 | tf_op jit(solution)/shard_map/all_gather | solution.py:48
  75.0 13.4 %reduce-scatter.19.cloned.1.call-done = bf16[32,64]{1,0:T(8,128)(2,1)} async-done(((bf16[128,64]{1,0:T(8,128)(2,1)}), bf16[32,64]{1,0:T(8,128)(2,1)}) %reduce-scatter.19.cloned.1.call-update) | async-done | bytes 4112 | tf_op jit(solution)/shard_map/reduce_scatter | solution.py:52
  88.4 3.1 scatter_custom_fusion
  97.0 39.9 %all-reduce.5 = (f32[64,64]{1,0:T(8,128)S(1)}, f32[64,64]{1,0:T(8,128)S(1)}) all-reduce(f32[64,64]{1,0:T(8,128)S(1)} %fusion.164, f32[64,64]{1,0:T(8,128)S(1)} %fusion.43), channel_id=1, replica_groups=mesh['row'=4,'col'=8] {'row','col'}, use_global_device_ids=true, to_apply=%region_2.3 | all-reduce | flops 8192 | bytes 65536 | tf_op jit(solution)/shard_map/psum | solution.py:72
  139.2 41.1 %psum.128 = f32[64,64]{1,0:T(8,128)S(1)} all-reduce(f32[64,64]{1,0:T(8,128)S(1)} %fusion.165), channel_id=1, replica_groups=mesh['row'=4,'col'=8] {'row','col'}, use_global_device_ids=true, to_apply=%region_4.5 | all-reduce | flops 4096 | bytes 32768 | tf_op jit(solution)/shard_map/psum | solution.py:82
  180.5 5.9 cholesky.104
  188.3 4.9 custom-call.10
  195.9 5.2 gather_fusion.5
  204.8 4.4 collective-permute-start.2
  210.6 4.3 collective-permute-done.3
  217.6 6.3 fusion.15
  223.8 28.6 %all-gather.9.cloned.1.call-done = bf16[64,8192]{0,1:T(8,128)(2,1)} async-done(((bf16[64,1024]{0,1:T(8,128)(2,1)}), bf16[64,8192]{0,1:T(8,128)(2,1)}) %all-gather.9.cloned.1.call-update) | async-done | bytes 1048592 | tf_op jit(solution)/shard_map/all_gather | solution.py:48
  255.7 3.1 fusion.156
  263.3 10.3 reduce-scatter.21.cloned.1.call-done
  273.6 3.1 scatter_custom_fusion.1
  282.4 39.9 %all-reduce.4 = (f32[64,64]{1,0:T(8,128)S(1)}, f32[64,64]{1,0:T(8,128)S(1)}) all-reduce(f32[64,64]{1,0:T(8,128)S(1)} %fusion.166, f32[64,64]{1,0:T(8,128)S(1)} %fusion.167), channel_id=1, replica_groups=mesh['row'=4,'col'=8] {'row','col'}, use_global_device_ids=true, to_apply=%region_9.0 | all-reduce | flops 8192 | bytes 65536 | tf_op jit(solution)/shard_map/psum | solution.py:72
  325.9 41.1 %psum.131 = f32[64,64]{1,0:T(8,128)S(1)} all-reduce(f32[64,64]{1,0:T(8,128)S(1)} %fusion.168), channel_id=1, replica_groups=mesh['row'=4,'col'=8] {'row','col'}, use_global_device_ids=true, to_apply=%region_11.0 | all-reduce | flops 4096 | bytes 32768 | tf_op jit(solution)/shard_map/psum | solution.py:82
  367.2 5.9 cholesky.115
  375.0 4.9 custom-call.11
  382.6 5.2 gather_fusion.8
  392.2 4.1 collective-permute-start.4
  398.1 4.4 collective-permute-done.5
  405.1 6.3 fusion.18
  411.4 27.5 %all-gather.11.cloned.1.call-done = bf16[64,8192]{0,1:T(8,128)(2,1)} async-done(((bf16[64,1024]{0,1:T(8,128)(2,1)}), bf16[64,8192]{0,1:T(8,128)(2,1)}) %all-gather.11.cloned.1.call-update) | async-done | bytes 1048592 | tf_op jit(solution)/shard_map/all_gather | solution.py:48
  442.1 3.1 fusion.155
  449.8 10.3 reduce-scatter.23.cloned.1.call-done
  468.9 39.9 %all-reduce.3 = (f32[64,64]{1,0:T(8,128)S(1)}, f32[64,64]{1,0:T(8,128)S(1)}) all-reduce(f32[64,64]{1,0:T(8,128)S(1)} %fusion.169, f32[64,64]{1,0:T(8,128)S(1)} %fusion.170), channel_id=1, replica_groups=mesh['row'=4,'col'=8] {'row','col'}, use_global_device_ids=true, to_apply=%region_14.0 | all-reduce | flops 8192 | bytes 65536 | tf_op jit(solution)/shard_map/psum | solution.py:72
  512.4 41.1 %psum.134 = f32[64,64]{1,0:T(8,128)S(1)} all-reduce(f32[64,64]{1,0:T(8,128)S(1)} %fusion.171), channel_id=1, replica_groups=mesh['row'=4,'col'=8] {'row','col'}, use_global_device_ids=true, to_apply=%region_16.0 | all-reduce | flops 4096 | bytes 32768 | tf_op jit(solution)/shard_map/psum | solution.py:82
  553.7 5.9 cholesky.126
  561.5 4.9 custom-call.12
  569.1 5.2 gather_fusion.11
  578.6 4.1 collective-permute-start.6
  584.9 4.0 collective-permute-done.7
  591.5 6.3 fusion.21
  597.8 27.5 %all-gather.13.cloned.1.call-done = bf16[64,8192]{0,1:T(8,128)(2,1)} async-done(((bf16[64,1024]{0,1:T(8,128)(2,1)}), bf16[64,8192]{0,1:T(8,128)(2,1)}) %all-gather.13.cloned.1.call-update) | async-done | bytes 1048592 | tf_op jit(solution)/shard_map/all_gather | solution.py:48
  628.6 3.1 fusion.154
  636.2 10.3 reduce-scatter.25.cloned.1.call-done
  655.4 39.9 %all-reduce.2 = (f32[64,64]{1,0:T(8,128)S(1)}, f32[64,64]{1,0:T(8,128)S(1)}) all-reduce(f32[64,64]{1,0:T(8,128)S(1)} %fusion.172, f32[64,64]{1,0:T(8,128)S(1)} %fusion.173), channel_id=1, replica_groups=mesh['row'=4,'col'=8] {'row','col'}, use_global_device_ids=true, to_apply=%region_19.0 | all-reduce | flops 8192 | bytes 65536 | tf_op jit(solution)/shard_map/psum | solution.py:72
  698.8 41.1 %psum.137 = f32[64,64]{1,0:T(8,128)S(1)} all-reduce(f32[64,64]{1,0:T(8,128)S(1)} %fusion.174), channel_id=1, replica_groups=mesh['row'=4,'col'=8] {'row','col'}, use_global_device_ids=true, to_apply=%region_21.0 | all-reduce | flops 4096 | bytes 32768 | tf_op jit(solution)/shard_map/psum | solution.py:82
  740.2 5.9 cholesky.137
  748.0 4.9 custom-call.13
  755.6 5.2 gather_fusion.14
  768.4 4.2 collective-permute-start.8
  774.7 3.5 collective-permute-done.9
  780.8 6.3 fusion.24
  787.1 25.1 %all-gather.15.cloned.1.call-done = bf16[64,8192]{0,1:T(8,128)(2,1)} async-done(((bf16[64,1024]{0,1:T(8,128)(2,1)}), bf16[64,8192]{0,1:T(8,128)(2,1)}) %all-gather.15.cloned.1.call-update) | async-done | bytes 1048592 | tf_op jit(solution)/shard_map/all_gather | solution.py:48
  815.5 3.1 fusion.153
  823.2 10.3 reduce-scatter.27.cloned.1.call-done
  842.3 39.9 %all-reduce.1 = (f32[64,64]{1,0:T(8,128)S(1)}, f32[64,64]{1,0:T(8,128)S(1)}) all-reduce(f32[64,64]{1,0:T(8,128)S(1)} %fusion.175, f32[64,64]{1,0:T(8,128)S(1)} %fusion.176), channel_id=1, replica_groups=mesh['row'=4,'col'=8] {'row','col'}, use_global_device_ids=true, to_apply=%region_24.0 | all-reduce | flops 8192 | bytes 65536 | tf_op jit(solution)/shard_map/psum | solution.py:72
  885.7 41.1 %psum.140 = f32[64,64]{1,0:T(8,128)S(1)} all-reduce(f32[64,64]{1,0:T(8,128)S(1)} %fusion.177), channel_id=1, replica_groups=mesh['row'=4,'col'=8] {'row','col'}, use_global_device_ids=true, to_apply=%region_26.0 | all-reduce | flops 4096 | bytes 32768 | tf_op jit(solution)/shard_map/psum | solution.py:82
  927.0 5.9 cholesky.148
  935.0 4.9 custom-call.14
  942.7 4.3 gather_fusion.17
  952.6 4.2 collective-permute-start.10
  964.4 6.3 fusion.27
  970.7 27.5 %all-gather.17.cloned.1.call-done = bf16[64,8192]{0,1:T(8,128)(2,1)} async-done(((bf16[64,1024]{0,1:T(8,128)(2,1)}), bf16[64,8192]{0,1:T(8,128)(2,1)}) %all-gather.17.cloned.1.call-update) | async-done | bytes 1048592 | tf_op jit(solution)/shard_map/all_gather | solution.py:48
  1007.8 11.6 %reduce-scatter.29.cloned.1.call-done = bf16[32,64]{1,0:T(8,128)(2,1)} async-done(((bf16[128,64]{1,0:T(8,128)(2,1)}), bf16[32,64]{1,0:T(8,128)(2,1)}) %reduce-scatter.29.cloned.1.call-update) | async-done | bytes 4112 | tf_op jit(solution)/shard_map/reduce_scatter | solution.py:52
  1028.0 39.9 %all-reduce = (f32[64,64]{1,0:T(8,128)S(1)}, f32[64,64]{1,0:T(8,128)S(1)}) all-reduce(f32[64,64]{1,0:T(8,128)S(1)} %fusion.178, f32[64,64]{1,0:T(8,128)S(1)} %fusion.179), channel_id=1, replica_groups=mesh['row'=4,'col'=8] {'row','col'}, use_global_device_ids=true, to_apply=%region_29.0 | all-reduce | flops 8192 | bytes 65536 | tf_op jit(solution)/shard_map/psum | solution.py:72
  1070.7 41.1 %psum.143 = f32[64,64]{1,0:T(8,128)S(1)} all-reduce(f32[64,64]{1,0:T(8,128)S(1)} %fusion.180), channel_id=1, replica_groups=mesh['row'=4,'col'=8] {'row','col'}, use_global_device_ids=true, to_apply=%region_31.34 | all-reduce | flops 4096 | bytes 32768 | tf_op jit(solution)/shard_map/psum | solution.py:82
  1112.1 5.9 cholesky.159
  1119.3 4.9 custom-call.15
  (279 shorter events, 207.0 us)
Async XLA Ops:
  7.2 60.0 %copy-start = (bf16[128,8192]{1,0:T(8,128)(2,1)S(1)}, bf16[128,8192]{1,0:T(8,128)(2,1)}, u32[]{:S(2)}) copy-start(bf16[128,8192]{1,0:T(8,128)(2,1)} %param.17) | copy-start | bytes 6291460
  7.2 14.6 %copy-start.26 = (s32[16,4]{0,1:T(4,128)S(1)}, s32[16,4]{0,1:T(4,128)}, u32[]{:S(2)}) copy-start(s32[16,4]{0,1:T(4,128)} %param.13) | copy-start | bytes 772
  7.2 14.8 %copy-start.27 = (f32[2]{0:T(128)S(1)}, f32[2]{0:T(128)}, u32[]{:S(2)}) copy-start(f32[2]{0:T(128)} %param.18) | copy-start | bytes 28
  7.2 60.0 %all-gather.7.cloned.1.call-start = ((), (), s32[]{:S(2)}) async-start(), calls=%async_computation.6 | async-start | bytes 2359296 | tf_op jit(solution)/shard_map/all_gather | solution.py:48
  14.9 73.5 %reduce-scatter.19.cloned.1.call-start = ((), (), s32[]{:S(2)}) async-start(), calls=%async_computation.12 | async-start | bytes 40960 | tf_op jit(solution)/shard_map/reduce_scatter | solution.py:52
  15.6 7.7 collective-permute-start
  20.5 5.8 collective-permute-start.1
  23.3 65.1 %copy-start.28 = (s32[32]{0:T(128)}, s32[32]{0:T(128)S(1)}, u32[]{:S(2)}) copy-start(s32[32]{0:T(128)S(1)} %compare_select_fusion.2) | copy-start | bytes 388
  70.4 182.1 %all-gather.9.cloned.1.call-start = ((), (), s32[]{:S(2)}) async-start(), calls=%async_computation.7 | async-start | bytes 2359296 | tf_op jit(solution)/shard_map/all_gather | solution.py:48
  91.4 5.0 copy-start.1
  137.8 0.8 copy-start.9
  194.9 15.8 %copy-start.14 = (bf16[64,2048]{1,0:T(8,128)(2,1)}, bf16[64,2048]{1,0:T(8,128)(2,1)S(1)}, u32[]{:S(2)}) copy-start(bf16[64,2048]{1,0:T(8,128)(2,1)S(1)} %get-tuple-element.42) | copy-start | bytes 786436
  202.9 70.7 %reduce-scatter.21.cloned.1.call-start = ((), (), s32[]{:S(2)}) async-start(), calls=%async_computation.13 | async-start | bytes 40960 | tf_op jit(solution)/shard_map/reduce_scatter | solution.py:52
  204.8 5.8 collective-permute-start.2
  209.2 5.7 collective-permute-start.3
  255.6 183.3 %all-gather.11.cloned.1.call-start = ((), (), s32[]{:S(2)}) async-start(), calls=%async_computation.8 | async-start | bytes 2359296 | tf_op jit(solution)/shard_map/all_gather | solution.py:48
  281.1 0.8 copy-start.2
  322.3 2.2 copy-start.16
  324.5 0.8 copy-start.10
  381.6 16.4 %copy-start.15 = (bf16[64,2048]{1,0:T(8,128)(2,1)}, bf16[64,2048]{1,0:T(8,128)(2,1)S(1)}, u32[]{:S(2)}) copy-start(bf16[64,2048]{1,0:T(8,128)(2,1)S(1)} %get-tuple-element.44) | copy-start | bytes 786436
  389.7 70.4 %reduce-scatter.23.cloned.1.call-start = ((), (), s32[]{:S(2)}) async-start(), calls=%async_computation.14 | async-start | bytes 40960 | tf_op jit(solution)/shard_map/reduce_scatter | solution.py:52
  392.2 5.9 collective-permute-start.4
  396.3 6.1 collective-permute-start.5
  442.1 183.3 %all-gather.13.cloned.1.call-start = ((), (), s32[]{:S(2)}) async-start(), calls=%async_computation.9 | async-start | bytes 2359296 | tf_op jit(solution)/shard_map/all_gather | solution.py:48
  467.5 0.8 copy-start.3
  508.7 3.6 copy-start.18
  508.8 3.6 copy-start.24
  511.0 0.8 copy-start.6
  568.1 16.8 %copy-start.13 = (bf16[64,2048]{1,0:T(8,128)(2,1)}, bf16[64,2048]{1,0:T(8,128)(2,1)S(1)}, u32[]{:S(2)}) copy-start(bf16[64,2048]{1,0:T(8,128)(2,1)S(1)} %get-tuple-element.46) | copy-start | bytes 786436
  576.1 70.4 %reduce-scatter.25.cloned.1.call-start = ((), (), s32[]{:S(2)}) async-start(), calls=%async_computation.15 | async-start | bytes 40960 | tf_op jit(solution)/shard_map/reduce_scatter | solution.py:52
  578.6 6.2 collective-permute-start.6
  582.8 6.1 collective-permute-start.7
  628.6 183.7 %all-gather.15.cloned.1.call-start = ((), (), s32[]{:S(2)}) async-start(), calls=%async_computation.10 | async-start | bytes 2359296 | tf_op jit(solution)/shard_map/all_gather | solution.py:48
  654.0 0.8 copy-start.4
  695.2 2.2 copy-start.22
  695.2 3.6 copy-start.20
  697.5 0.8 copy-start.7
  752.9 10.7 copy-start.17
  754.6 20.1 %copy-start.12 = (bf16[64,2048]{1,0:T(8,128)(2,1)}, bf16[64,2048]{1,0:T(8,128)(2,1)S(1)}, u32[]{:S(2)}) copy-start(bf16[64,2048]{1,0:T(8,128)(2,1)S(1)} %get-tuple-element.48) | copy-start | bytes 786436
  754.6 19.5 %copy-start.19 = (f32[64,64]{1,0:T(8,128)S(1)}, f32[64,64]{1,0:T(8,128)}, u32[]{:S(2)}) copy-start(f32[64,64]{1,0:T(8,128)} %copy-done.18) | copy-start | bytes 49156
  762.7 70.8 %reduce-scatter.27.cloned.1.call-start = ((), (), s32[]{:S(2)}) async-start(), calls=%async_computation.16 | async-start | bytes 40960 | tf_op jit(solution)/shard_map/reduce_scatter | solution.py:52
  764.3 0.8 copy-start.25
  768.4 6.3 collective-permute-start.8
  772.5 5.6 collective-permute-start.9
  815.5 182.7 %all-gather.17.cloned.1.call-start = ((), (), s32[]{:S(2)}) async-start(), calls=%async_computation.11 | async-start | bytes 2359296 | tf_op jit(solution)/shard_map/all_gather | solution.py:48
  840.9 0.8 copy-start.5
  884.3 0.8 copy-start.8
  939.8 10.5 copy-start.23
  939.9 10.5 copy-start.21
  948.9 70.5 %reduce-scatter.29.cloned.1.call-start = ((), (), s32[]{:S(2)}) async-start(), calls=%async_computation.17 | async-start | bytes 40960 | tf_op jit(solution)/shard_map/reduce_scatter | solution.py:52
  952.6 7.2 collective-permute-start.10
  956.8 5.9 collective-permute-start.11
  1024.8 2.7 copy-start.11
Sparse Core Ops, SparseCore 0:
  15.0 52.1 all-gather.6
  70.5 17.8 reduce-scatter.18
  203.0 49.3 all-gather.8
  255.8 17.8 reduce-scatter.20
  389.8 49.0 all-gather.10
  442.2 17.8 reduce-scatter.22
  576.2 49.0 all-gather.12
  628.7 17.8 reduce-scatter.24
  762.8 49.4 all-gather.14
  815.6 17.8 reduce-scatter.26
  949.0 49.1 all-gather.16
  1001.5 17.8 reduce-scatter.28
where the time goes:
time: 1150 us; the launch traced here: 1130 us
  blocking collectives  486 us (42%)
  waiting for transfers between devices  256 us (22%)
  other arithmetic  149 us (13%)
  local copies, waits for them, and re-layouts  106 us (9%)
  matrix products  84.9 us (7%)
  starting transfers between devices  35.1 us (3%)
  between operations  16.7 us (1%)
    psum x6, blocking collectives, local(): lax.psum(contract_rows(residual, residual), ('row', 'col')) / total_rows  247 us
    psum x6, blocking collectives, local(): lax.psum((contract_rows(applied, current), contract_rows(applied, previou...  239 us
    all_gather x6, waiting for transfers between devices, local(): lax.all_gather(slot_values, 'col', axis=1, tiled=True)  167 us
    reduce_scatter x6, waiting for transfers between devices, local(): lax.psum_scatter(partial_sum.astype(jnp.bfloat16), 'row', scatter_dimensi...  66.2 us
    another operation x18, other arithmetic, local(): factor = jnp.linalg.cholesky(gram_matrix)  39.3 us
    dot_general x6, matrix products, local(): jnp.einsum('vikb,mikab->mvia', picked, struct_blocks, preferred_element_t...  37.5 us
    ppermute x12, starting transfers between devices, from_behind(): return lax.ppermute(shard, axis, pairs)  34.6 us
    another operation x6, other arithmetic, local(): lax.linalg.triangular_solve(factor, residual, left_side=True, lower=True)  29.4 us
  transfers between devices with their start and end apart: 24, of which 19 were waited for; matrix products, arithmetic and copies ran while one was open for 10% of the time, Pallas kernels for 0%

commit v1 on v0

v1 whole, which is shorter than its diff:
```python
import functools

import jax
import jax.numpy as jnp
from jax import lax
from jax.experimental import pallas as pl
from jax.experimental.pallas import tpu as pltpu
from jax.sharding import PartitionSpec as P

STEPS = 6
AXES = ("row", "col")
VMEM = pl.BlockSpec(memory_space=pltpu.VMEM)
SMEM = pl.BlockSpec(memory_space=pltpu.SMEM)
F32 = jnp.float32
BF16 = jnp.bfloat16
LIMIT = 40 * 1024 * 1024


def exact(left, right):
    return lax.dot_general(
        left, right, (((1,), (0,)), ((), ())), precision=lax.Precision.HIGHEST, preferred_element_type=F32
    )


def exact_rows(left, right):
    return lax.dot_general(
        left, right, (((1,), (1,)), ((), ())), precision=lax.Precision.HIGHEST, preferred_element_type=F32
    )


def rows(left, right):
    return lax.dot_general(left, right, (((1,), (1,)), ((), ())), preferred_element_type=F32)


def combine_kernel(rates, rim, wet, start, blocks, mixed, pick, place, halo):
    size = blocks.shape[-1]
    for k in range(blocks.shape[2]):
        whole = (
            blocks[0, 0, k].astype(F32)
            + rates[0] * blocks[1, 0, k].astype(F32)
            - rates[1] * blocks[2, 0, k].astype(F32)
        ).T
        high = whole.astype(BF16)
        mixed[0, k * size : (k + 1) * size, :size] = high
        mixed[0, k * size : (k + 1) * size, size:] = (whole - high.astype(F32)).astype(BF16)

    @pl.when(pl.program_id(0) == 0)
    def _():
        index = lax.broadcasted_iota(jnp.int32, pick.shape, 0)
        pick[...] = jnp.where(index == rim[...], 1.0, 0.0).astype(BF16)
        index = lax.broadcasted_iota(jnp.int32, place.shape, 1)
        place[...] = jnp.where(index == wet[...], 1.0, 0.0).astype(F32)
        halo[...] = jnp.dot(start[...].astype(BF16), pick[...], preferred_element_type=F32)


def combine(rates, rim, wet, start, blocks):
    _, count, nnz, size, _ = blocks.shape
    vectors, width = start.shape
    whole = lambda shape: pl.BlockSpec(shape, lambda i: (0,) * len(shape))
    return pl.pallas_call(
        combine_kernel,
        grid=(count,),
        in_specs=[
            SMEM,
            whole(rim.shape),
            whole(wet.shape),
            whole(start.shape),
            pl.BlockSpec((3, 1, nnz, size, size), lambda i: (0, i, 0, 0, 0)),
        ],
        out_specs=[
            pl.BlockSpec((1, nnz * size, 2 * size), lambda i: (i, 0, 0)),
            whole((width, rim.shape[1])),
            whole((wet.shape[0], width)),
            whole((vectors, rim.shape[1])),
        ],
        out_shape=[
            jax.ShapeDtypeStruct((count, nnz * size, 2 * size), BF16),
            jax.ShapeDtypeStruct((width, rim.shape[1]), BF16),
            jax.ShapeDtypeStruct((wet.shape[0], width), F32),
            jax.ShapeDtypeStruct((vectors, rim.shape[1]), F32),
        ],
        compiler_params=pltpu.CompilerParams(vmem_limit_bytes=LIMIT),
        name="combine",
    )(rates, rim, wet, start, blocks)


def spread_kernel(count, slots, start, mass, spread, part, onehot, values):
    @pl.when(pl.program_id(0) == 0)
    def _():
        slot = lax.broadcasted_iota(jnp.int32, slots.shape, 1)
        live = jnp.where(slot < count[0], slots[...], -1)
        index = lax.broadcasted_iota(jnp.int32, onehot.shape, 0)
        onehot[...] = jnp.where(index == live, 1.0, 0.0).astype(BF16)
        values[...] = start[...].astype(BF16)

    width, vectors = onehot.shape[0], values.shape[0]
    halves = []
    for h in range(2):
        own = mass[:, 0, h].reshape(-1, mass.shape[-1])
        spread[h] = rows(own, onehot[...]).astype(BF16)
        halves.append(rows(spread[h], values[...]))
    part[:, :vectors] = halves[0]
    part[:, vectors:] = halves[1]


def spread_mass(count, slots, start, mass):
    n_col, n_row, _, half, wcap = mass.shape
    vectors, width = start.shape
    size = n_col * half
    return pl.pallas_call(
        spread_kernel,
        grid=(n_row,),
        in_specs=[
            SMEM,
            pl.BlockSpec(slots.shape, lambda r: (0, 0)),
            pl.BlockSpec(start.shape, lambda r: (0, 0)),
            pl.BlockSpec((n_col, 1, 2, half, wcap), lambda r: (0, r, 0, 0, 0)),
        ],
        out_specs=[
            pl.BlockSpec((2, size, width), lambda r: (0, r, 0)),
            pl.BlockSpec((size, 2 * vectors), lambda r: (r, 0)),
        ],
        out_shape=[
            jax.ShapeDtypeStruct((2, n_row * size, width), BF16),
            jax.ShapeDtypeStruct((n_row * size, 2 * vectors), F32),
        ],
        scratch_shapes=[pltpu.VMEM((width, wcap), BF16), pltpu.VMEM((vectors, width), BF16)],
        compiler_params=pltpu.CompilerParams(vmem_limit_bytes=LIMIT),
        name="spread",
    )(count, slots, start, mass)


def small_matrices(total, gram, inner, factor_t, mix, coef):
    n = gram.shape[0] // 2
    scale = 1.0 / total
    aa = gram[:n, :n] * scale
    self_ = gram[:n, n:] * scale
    prev = gram[n:, :n] * scale
    cc = gram[n:, n:] * scale
    cp = inner[:, :n]
    pp = inner[:, n:]
    t_c = self_ - exact(self_, cc) - exact_rows(prev, cp)
    t_p = prev - exact(self_, cp) - exact(prev, pp)
    t_a = aa - exact_rows(self_, self_) - exact_rows(prev, prev)
    matrix = t_a - exact_rows(t_c, self_) - exact_rows(t_p, prev)
    matrix = 0.5 * (matrix + matrix.T)
    row_id = lax.broadcasted_iota(jnp.int32, (n, 2 * n), 0)
    lane_id = lax.broadcasted_iota(jnp.int32, (n, 2 * n), 1)
    factor_t[:, :n] = matrix
    factor_t[:, n:] = jnp.where(row_id == lane_id, 1.0, 0.0).astype(F32)[:, :n]
    work = [factor_t[g * 8 : (g + 1) * 8, :] for g in range(n // 8)]
    sub = lax.broadcasted_iota(jnp.int32, (8, 1), 0)
    for j in range(n):
        g, s = divmod(j, 8)
        pivot_row = work[g][s : s + 1, :]
        scaled = pivot_row / pivot_row[:, j : j + 1]
        for i in range(g, n // 8):
            column = work[i][:, j : j + 1]
            if i == g:
                column = jnp.where(sub > s, column, 0.0)
            work[i] = work[i] - column * scaled
    reduced = jnp.concatenate(work, 0)
    diagonal = jnp.sum(jnp.where(row_id == lane_id, reduced, 0.0), 1, keepdims=True)
    reduced = reduced * lax.rsqrt(diagonal)
    factor_t[...] = reduced
    inverse = factor_t[:, n:]
    mix[:, :n] = inverse
    mix[:, n : 2 * n] = -exact(inverse, self_)
    mix[:, 2 * n :] = -exact(inverse, prev)
    coef[0] = self_
    coef[1] = prev
    upper = jnp.where(row_id <= lane_id, reduced, 0.0)
    coef[2] = upper.T[:n, :]
    return exact(inverse, t_c), cc


def advance_kernel(first, total, *refs):
    it = iter(refs)
    ids, rates = next(it), next(it)
    if first:
        start = next(it)
    else:
        gram_in, inner, stack, edges, wet_held = (next(it) for _ in range(5))
    arrived, below, above, mixed, pick, place, spread = (next(it) for _ in range(7))
    stack_out, edges_out, wet_out, gram_out, halo_out, part_out = (next(it) for _ in range(6))
    if not first:
        inner_out, coef = next(it), next(it)
    extended, split = next(it), next(it)
    if not first:
        factor_t, mix, edge_all = (next(it) for _ in range(3))
    n = stack_out.shape[0] // 3
    width = stack_out.shape[1]
    size = below.shape[1]
    summed = jnp.sum(arrived[...].astype(F32), 0)
    half = summed.shape[0]
    if first:
        current = start[...]
        stack_out[n : 2 * n, :] = current
        stack_out[2 * n :, :] = jnp.zeros_like(current)
        edges_out[:n, :size] = below[...]
        edges_out[:n, size:] = above[...]
        edges_out[n:, :] = jnp.zeros_like(edges_out[n:, :])
        wet_out[:half, :n] = summed[:, :n]
        wet_out[half:, :n] = summed[:, n:]
        wet_out[:, n:] = jnp.zeros_like(wet_out[:, n:])
    else:
        cp, cc = small_matrices(total, gram_in, inner, factor_t, mix, coef)
        inner_out[:, :n] = cp
        inner_out[:, n:] = cc
        current = exact(mix[...], stack[...])
        stack_out[n : 2 * n, :] = current
        stack_out[2 * n :, :] = stack[n : 2 * n, :]
        edge_all[:n, :size] = below[...]
        edge_all[:n, size:] = above[...]
        edge_all[n:, :] = edges[...]
        edges_out[:n, :] = exact(mix[...], edge_all[...])
        edges_out[n:, :] = edges[:n, :]
        fresh = exact_rows(jnp.concatenate([summed[:, :n], summed[:, n:]], 0), mix[:, :n])
        fresh = fresh + exact_rows(wet_held[:, :n], mix[:, n : 2 * n])
        fresh = fresh + exact_rows(wet_held[:, n:], mix[:, 2 * n :])
        wet_out[:, :n] = fresh
        wet_out[:, n:] = wet_held[:, :n]
    count = width // size
    for i in range(count):
        extended[i] = stack_out[n : 2 * n, i * size : (i + 1) * size].astype(BF16)
    extended[count] = edges_out[:n, :size].astype(BF16)
    extended[count + 1] = edges_out[:n, size:].astype(BF16)
    force = wet_out[:, :n].T * rates[1]
    for i in range(count):
        picked = jnp.concatenate([extended[ids[i, k]] for k in range(ids.shape[1])], 1)
        both = jnp.dot(picked, mixed[i], preferred_element_type=F32)
        lanes = slice(i * size, (i + 1) * size)
        applied = both[:, :size] + both[:, size:] - exact(force, place[:, lanes])
        stack_out[:n, lanes] = applied
        high = applied.astype(BF16)
        split[:n, lanes] = high
        split[n:, lanes] = (applied - high.astype(F32)).astype(BF16)
    products = exact_rows(stack_out[:n, :], stack_out[...])
    gram_out[:n, :] = products[:, : 2 * n]
    gram_out[n:, :n] = products[:, 2 * n :]
    gram_out[n:, n:] = exact_rows(stack_out[n : 2 * n, :], stack_out[n : 2 * n, :])
    rim = jnp.dot(split[...], pick[...], preferred_element_type=F32)
    halo_out[...] = rim[:n] + rim[n:]
    tops = rows(spread[0], split[...])
    tops = tops + pltpu.roll(tops, n, 1)
    ends = rows(spread[1], split[...])
    ends = ends + pltpu.roll(ends, n, 1)
    lane = lax.broadcasted_iota(jnp.int32, tops.shape, 1)
    part_out[...] = jnp.where(lane < n, tops, ends).astype(part_out.dtype)


def advance(first, total, ids, rates, state, arrived, below, above, fixed):
    mixed, pick, place, spread = fixed
    vectors, size = below.shape
    width = pick.shape[0]
    wets = place.shape[0]
    shapes = [
        jax.ShapeDtypeStruct((3 * vectors, width), F32),
        jax.ShapeDtypeStruct((2 * vectors, 2 * size), F32),
        jax.ShapeDtypeStruct((wets, 2 * vectors), F32),
        jax.ShapeDtypeStruct((2 * vectors, 2 * vectors), F32),
        jax.ShapeDtypeStruct((vectors, size), F32),
        jax.ShapeDtypeStruct((spread.shape[1], 2 * vectors), F32),
    ]
    scratch = [
        pltpu.VMEM((width // size + 2, vectors, size), BF16),
        pltpu.VMEM((2 * vectors, width), BF16),
    ]
    if not first:
        shapes += [
            jax.ShapeDtypeStruct((vectors, 2 * vectors), F32),
            jax.ShapeDtypeStruct((3, vectors, vectors), F32),
        ]
        scratch += [
            pltpu.VMEM((vectors, 2 * vectors), F32),
            pltpu.VMEM((vectors, 3 * vectors), F32),
            pltpu.VMEM((3 * vectors, 2 * size), F32),
        ]
    return pl.pallas_call(
        functools.partial(advance_kernel, first, total),
        in_specs=[SMEM, SMEM] + [VMEM] * (len(state) + 7),
        out_specs=[VMEM] * len(shapes),
        out_shape=shapes,
        scratch_shapes=scratch,
        compiler_params=pltpu.CompilerParams(vmem_limit_bytes=LIMIT),
        name="advance",
    )(ids, rates, *state, arrived, below, above, mixed, pick, place, spread)


def finish_kernel(total, gram_in, inner, stack, out, coef, factor_t, mix):
    small_matrices(total, gram_in, inner, factor_t, mix, coef)
    out[...] = exact(mix[...], stack[...])


def finish(total, gram, inner, stack):
    vectors = gram.shape[0] // 2
    return pl.pallas_call(
        functools.partial(finish_kernel, total),
        in_specs=[VMEM] * 3,
        out_specs=[VMEM] * 2,
        out_shape=[
            jax.ShapeDtypeStruct((vectors, stack.shape[1]), F32),
            jax.ShapeDtypeStruct((3, vectors, vectors), F32),
        ],
        scratch_shapes=[
            pltpu.VMEM((vectors, 2 * vectors), F32),
            pltpu.VMEM((vectors, 3 * vectors), F32),
        ],
        compiler_params=pltpu.CompilerParams(vmem_limit_bytes=LIMIT),
        name="finish",
    )(gram, inner, stack)


def local(n_row, n_col, start_block, struct_blocks, block_ids, rim_rows, wet_slots, wet_counts, added_mass, rates):
    peers = n_row * n_col
    vectors, width = start_block.shape
    total = float(width * peers)
    wcap = wet_slots.shape[0]
    wets = added_mass.shape[0] // n_row

    def exchange(parts):
        return lax.all_to_all(parts, AXES, 0, 0, tiled=True)

    def neighbours(halo):
        up = [(i, i + 1) for i in range(peers - 1)]
        down = [(i + 1, i) for i in range(peers - 1)]
        return lax.ppermute(halo, AXES, up), lax.ppermute(halo, AXES, down)

    def summed(gram):
        lines = gram.shape[0] // peers
        mine = exchange(gram.reshape(peers, lines, -1)).sum(0)
        return exchange(jnp.broadcast_to(mine[None], (peers, *mine.shape))).reshape(gram.shape)

    def pressure(part):
        return exchange(part.reshape(peers, wets // 2, 2 * vectors))

    blocks = added_mass.reshape(-1, n_col, wcap).transpose(1, 0, 2)
    mass = lax.all_to_all(blocks, "col", 0, 0, tiled=True)
    mass = mass.reshape(n_col, n_row, 2, wets // 2, wcap)
    mixed, pick, place, halo = combine(
        rates, rim_rows[None, :], wet_slots[:wets, None], start_block, struct_blocks
    )
    spread, part = spread_mass(wet_counts, wet_slots[None, :], start_block, mass)
    fixed = (mixed, pick, place, spread)
    coefficients = []
    state = (start_block,)
    for number in range(STEPS):
        below, above = neighbours(halo)
        arrived = pressure(part)
        outs = advance(number == 0, total, block_ids, rates, state, arrived, below, above, fixed)
        stack, edges, wet_held, gram, halo, part = outs[:6]
        if number == 0:
            inner = jnp.zeros((vectors, 2 * vectors), F32)
        else:
            inner = outs[6]
            coefficients.append(outs[7])
        gram = summed(gram)
        state = (gram, inner, stack, edges, wet_held)
    final, coef = finish(total, gram, inner, stack)
    coefficients.append(coef)
    return final, jnp.stack(coefficients)


def solution(mesh):
    return jax.shard_map(
        functools.partial(local, mesh.shape["row"], mesh.shape["col"]),
        mesh=mesh,
        in_specs=(
            P(None, AXES),
            P(None, AXES, None, None, None),
            P(AXES, None),
            P(AXES),
            P(AXES),
            P(AXES),
            P("col", "row"),
            P(),
        ),
        out_specs=(P(None, AXES), P()),
        check_vma=False,
    )
```

time: 1150 us -> 428 us (0.37)
  blocking collectives: 486 us -> 115 us
  waiting for transfers between devices: 256 us -> 84 us
  other arithmetic: 149 us -> 0.26 us
  Pallas kernels: 0 us -> 99.5 us
  matrix products: 84.9 us -> 0 us
  local copies, waits for them, and re-layouts: 106 us -> 50.1 us
  starting transfers between devices: 35.1 us -> 69.2 us
  between operations: 16.7 us -> 1.85 us
    psum x12 -> x0, blocking collectives: 486 us -> none  [the longest x6 247 us: local(): lax.psum(contract_rows(residual, residual), ('row', 'col')) / total_rows]
    all_gather x6 -> x0, waiting for transfers between devices: 167 us -> none  [local(): lax.all_gather(slot_values, 'col', axis=1, tiled=True)]
    all_to_all x0 -> x10, blocking collectives: none -> 115 us  [exchange(): return lax.all_to_all(parts, AXES, 0, 0, tiled=True)]
    pallas_call x0 -> x9, Pallas kernels: none -> 99.5 us  [the longest x6 72.8 us: advance(): pl.pallas_call(functools.partial(advance_kernel, first, total), in_specs=...]
    another operation x43 -> x0, other arithmetic: 78.9 us -> none  [the longest x18 39.3 us: local(): factor = jnp.linalg.cholesky(gram_matrix)]
    all_to_all x0 -> x9, waiting for transfers between devices: none -> 76.8 us  [the longest x1 47.6 us: local(): mass = lax.all_to_all(blocks, 'col', 0, 0, tiled=True)]
    dot_general x42 -> x0, matrix products: 74.2 us -> none  [the longest x6 37.5 us: local(): jnp.einsum('vikb,mikab->mvia', picked, struct_blocks, preferred_element_t...]
    reduce_scatter x6 -> x0, waiting for transfers between devices: 66.2 us -> none  [local(): lax.psum_scatter(partial_sum.astype(jnp.bfloat16), 'row', scatter_dimensi...]
  transfers between devices with their start and end apart: 24 -> 21, of which waited for: 19 -> 14; matrix products, arithmetic and copies ran while one was open for 10% -> 0% of each run, Pallas kernels for 0% -> 1%
where the time goes in v1:
time: 428 us; the launch traced here: 419 us
  blocking collectives  115 us (27%)
  Pallas kernels  99.5 us (23%)
  waiting for transfers between devices  84 us (20%)
  starting transfers between devices  69.2 us (16%)
  local copies, waits for them, and re-layouts  50.1 us (12%)
    all_to_all x10, blocking collectives, exchange(): return lax.all_to_all(parts, AXES, 0, 0, tiled=True)  115 us
    pallas_call x6, Pallas kernels, advance(): pl.pallas_call(functools.partial(advance_kernel, first, total), in_specs=...  72.8 us
    all_to_all x1, waiting for transfers between devices, local(): mass = lax.all_to_all(blocks, 'col', 0, 0, tiled=True)  47.6 us
    unnamed x64, local copies, waits for them, and re-layouts  45.5 us
    ppermute x12, starting transfers between devices, neighbours(): return (lax.ppermute(halo, AXES, up), lax.ppermute(halo, AXES, down))  36.3 us
    all_to_all x8, waiting for transfers between devices, exchange(): return lax.all_to_all(parts, AXES, 0, 0, tiled=True)  29.3 us
    all_to_all x8, starting transfers between devices, exchange(): return lax.all_to_all(parts, AXES, 0, 0, tiled=True)  25.4 us
    pallas_call x1, Pallas kernels, spread_mass(): pl.pallas_call(spread_kernel, grid=(n_row,), in_specs=[SMEM, pl.BlockSpec...  14.6 us
  transfers between devices with their start and end apart: 21, of which 14 were waited for; matrix products, arithmetic and copies ran while one was open for 0% of the time, Pallas kernels for 1%

profile of v1, /device:TPU:0, one launch (start us, length us, event | category | flops | bytes accessed | tf_op | source)
XLA Modules:
  0.0 419.4 jit_solution(9456385115950721563)
XLA Ops:
  0.6 3.2 copy.20
  3.8 7.4 %all-to-all-start = ((bf16[8,128,1024]{2,1,0:T(8,128)(2,1)}), bf16[8,128,1024]{2,1,0:T(8,128)(2,1)S(1)}, u32[]{:S(2)}, u32[]{:S(2)}) async-start(bf16[8,128,1024]{2,1,0:T(8,128)(2,1)} %bitcast.56), calls=%async_computation | async-start | bytes 4194304 | tf_op jit(solution)/shard_map/all_to_all | solution.py:338
  11.9 47.6 %all-to-all-done = bf16[8,128,1024]{2,1,0:T(8,128)(2,1)S(1)} async-done(((bf16[8,128,1024]{2,1,0:T(8,128)(2,1)}), bf16[8,128,1024]{2,1,0:T(8,128)(2,1)S(1)}, u32[]{:S(2)}, u32[]{:S(2)}) %all-to-all-start) | async-done | bytes 2097184 | tf_op jit(solution)/shard_map/all_to_all | solution.py:338
  59.4 14.6 %spread.1 = (bf16[2,512,2048]{2,1,0:T(8,128)(2,1)S(1)}, f32[512,128]{1,0:T(8,128)}) custom-call(s32[1]{0:T(128)S(6)} %copy.26.count, s32[1,1024]{1,0:T(1,128)S(1)} %bitcast.54, f32[64,2048]{1,0:T(8,128)S(1)} %copy-done.15, bf16[8,4,2,16,1024]{4,3,2,1,0:T(8,128)(2,1)S(1)} %bitcast.42), custom_call_target="tpu_custom_call" | custom-call | tf_op jit(solution)/shard_map/spread/pallas_call | solution.py:110
  74.1 2.0 copy-done
  76.1 3.7 all-to-all-start.1
  79.9 2.8 copy-done.14
  82.7 3.9 combine.1
  86.6 1.9 copy-done.7
  89.9 4.5 %collective-permute-start = (f32[64,128]{1,0:T(8,128)S(1)}, f32[64,128]{1,0:T(8,128)S(1)}, u32[]{:S(2)}, u32[]{:S(2)}) collective-permute-start(f32[64,128]{1,0:T(8,128)S(1)} %get-tuple-element.53), channel_id=1, source_target_pairs={{0,1},{1,2},{2,3},{3,4},{4,5},{5,6},{6,7},{7,8},{8,9},{9,10},{10,1... | collective-permute-start | bytes 98312 | tf_op jit(solution)/shard_map/ppermute | solution.py:327
  94.5 1.5 collective-permute-done.refs_4_
  96.0 2.2 copy-done.1
  98.2 2.2 copy-done.8
  100.4 5.8 %advance.6 = (f32[192,2048]{1,0:T(8,128)S(1)}, f32[128,256]{1,0:T(8,128)S(1)}, f32[32,128]{1,0:T(8,128)S(1)}, f32[128,128]{1,0:T(8,128)S(1)}, f32[64,128]{1,0:T(8,128)S(1)}, /*index=5*/f32[512,128]{1,0:T(8,128)}) custom-call(s32[16,4]{1,0:T(8,128)S(1)} %copy.17.refs_0_, f32[2]{0:T(128)S(1)} %copy-done.24, f32[64,2048]{1,0:T(8,128)S(1)} %copy-done.15, ...), custom_call_target="tpu_custom_call" | custom-call | tf_op jit(solution)/shard_map/advance/pallas_call | solution.py:279
  107.3 16.5 %all_to_all.95 = f32[32,4,128]{2,1,0:T(4,128)S(1)} all-to-all(f32[32,4,128]{2,1,0:T(4,128)S(1)} %bitcast.53), channel_id=1, replica_groups=mesh['row'=4,'col'=8] {'row','col'}, dimensions={0} | all-to-all | bytes 131072 | tf_op jit(solution)/shard_map/all_to_all | solution.py:322
  123.9 9.0 %all_to_all.96 = f32[32,4,128]{2,1,0:T(4,128)S(1)} all-to-all(f32[32,4,128]{2,1,0:T(4,128)S(1)} %broadcast_in_dim.23), channel_id=1, replica_groups=mesh['row'=4,'col'=8] {'row','col'}, dimensions={0} | all-to-all | bytes 131072 | tf_op jit(solution)/shard_map/all_to_all | solution.py:322
  132.9 2.6 all-to-all-start.4
  136.8 4.8 %collective-permute-start.2 = (f32[64,128]{1,0:T(8,128)S(1)}, f32[64,128]{1,0:T(8,128)S(1)}, u32[]{:S(2)}, u32[]{:S(2)}) collective-permute-start(f32[64,128]{1,0:T(8,128)S(1)} %get-tuple-element.63), channel_id=1, source_target_pairs={{0,1},{1,2},{2,3},{3,4},{4,5},{5,6},{6,7},{7,8},{8,9},{9,10},{10,1... | collective-permute-start | bytes 98312 | tf_op jit(solution)/shard_map/ppermute | solution.py:327
  142.9 3.2 all-to-all-done.4.refs_7_
  146.1 2.2 copy-done.2
  148.3 2.2 copy-done.9
  150.5 1.4 copy-done.21
  151.9 13.4 %advance.7 = (f32[192,2048]{1,0:T(8,128)S(1)}, f32[128,256]{1,0:T(8,128)S(1)}, f32[32,128]{1,0:T(8,128)S(1)}, f32[128,128]{1,0:T(8,128)S(1)}, f32[64,128]{1,0:T(...) custom-call(s32[16,4]{1,0:T(8,128)S(1)} %copy.17.refs_0_, f32[2]{0:T(128)S(1)} %copy-done.24, ...), custom_call_target="tpu_custom_call" | custom-call | tf_op jit(solution)/shard_map/advance/pallas_call | solution.py:279
  165.3 13.3 %all_to_all.97 = f32[32,4,128]{2,1,0:T(4,128)S(1)} all-to-all(f32[32,4,128]{2,1,0:T(4,128)S(1)} %bitcast.49), channel_id=1, replica_groups=mesh['row'=4,'col'=8] {'row','col'}, dimensions={0} | all-to-all | bytes 131072 | tf_op jit(solution)/shard_map/all_to_all | solution.py:322
  178.6 9.0 %all_to_all.98 = f32[32,4,128]{2,1,0:T(4,128)S(1)} all-to-all(f32[32,4,128]{2,1,0:T(4,128)S(1)} %broadcast_in_dim.25), channel_id=1, replica_groups=mesh['row'=4,'col'=8] {'row','col'}, dimensions={0} | all-to-all | bytes 131072 | tf_op jit(solution)/shard_map/all_to_all | solution.py:322
  187.6 2.6 all-to-all-start.7
  191.5 4.8 %collective-permute-start.4 = (f32[64,128]{1,0:T(8,128)S(1)}, f32[64,128]{1,0:T(8,128)S(1)}, u32[]{:S(2)}, u32[]{:S(2)}) collective-permute-start(f32[64,128]{1,0:T(8,128)S(1)} %get-tuple-element.70), channel_id=1, source_target_pairs={{0,1},{1,2},{2,3},{3,4},{4,5},{5,6},{6,7},{7,8},{8,9},{9,10},{10,1... | collective-permute-start | bytes 98312 | tf_op jit(solution)/shard_map/ppermute | solution.py:327
  197.6 3.2 all-to-all-done.7.refs_7_
  200.8 2.2 copy-done.3
  203.0 2.2 copy-done.10
  205.2 13.4 %advance.8 = (f32[192,2048]{1,0:T(8,128)S(1)}, f32[128,256]{1,0:T(8,128)S(1)}, f32[32,128]{1,0:T(8,128)S(1)}, f32[128,128]{1,0:T(8,128)S(1)}, f32[64,128]{1,0:T(...) custom-call(s32[16,4]{1,0:T(8,128)S(1)} %copy.17.refs_0_, f32[2]{0:T(128)S(1)} %copy-done.24, ...), custom_call_target="tpu_custom_call" | custom-call | tf_op jit(solution)/shard_map/advance/pallas_call | solution.py:279
  219.8 13.3 %all_to_all.99 = f32[32,4,128]{2,1,0:T(4,128)S(1)} all-to-all(f32[32,4,128]{2,1,0:T(4,128)S(1)} %bitcast.50), channel_id=1, replica_groups=mesh['row'=4,'col'=8] {'row','col'}, dimensions={0} | all-to-all | bytes 131072 | tf_op jit(solution)/shard_map/all_to_all | solution.py:322
  233.1 9.0 %all_to_all.100 = f32[32,4,128]{2,1,0:T(4,128)S(1)} all-to-all(f32[32,4,128]{2,1,0:T(4,128)S(1)} %broadcast_in_dim.26), channel_id=1, replica_groups=mesh['row'=4,'col'=8] {'row','col'}, dimensions={0} | all-to-all | bytes 131072 | tf_op jit(solution)/shard_map/all_to_all | solution.py:322
  242.1 2.6 all-to-all-start.10
  246.0 5.0 %collective-permute-start.6 = (f32[64,128]{1,0:T(8,128)S(1)}, f32[64,128]{1,0:T(8,128)S(1)}, u32[]{:S(2)}, u32[]{:S(2)}) collective-permute-start(f32[64,128]{1,0:T(8,128)S(1)} %get-tuple-element.77), channel_id=1, source_target_pairs={{0,1},{1,2},{2,3},{3,4},{4,5},{5,6},{6,7},{7,8},{8,9},{9,10},{10,1... | collective-permute-start | bytes 98312 | tf_op jit(solution)/shard_map/ppermute | solution.py:327
  252.1 3.2 all-to-all-done.10.refs_7_
  255.3 2.2 copy-done.4
  257.5 2.2 copy-done.11
  259.7 1.4 copy-done.17
  261.1 13.4 %advance.9 = (f32[192,2048]{1,0:T(8,128)S(1)}, f32[128,256]{1,0:T(8,128)S(1)}, f32[32,128]{1,0:T(8,128)S(1)}, f32[128,128]{1,0:T(8,128)S(1)}, f32[64,128]{1,0:T(...) custom-call(s32[16,4]{1,0:T(8,128)S(1)} %copy.17.refs_0_, f32[2]{0:T(128)S(1)} %copy-done.24, ...), custom_call_target="tpu_custom_call" | custom-call | tf_op jit(solution)/shard_map/advance/pallas_call | solution.py:279
  275.7 13.3 %all_to_all.101 = f32[32,4,128]{2,1,0:T(4,128)S(1)} all-to-all(f32[32,4,128]{2,1,0:T(4,128)S(1)} %bitcast.51), channel_id=1, replica_groups=mesh['row'=4,'col'=8] {'row','col'}, dimensions={0} | all-to-all | bytes 131072 | tf_op jit(solution)/shard_map/all_to_all | solution.py:322
  289.0 9.0 %all_to_all.102 = f32[32,4,128]{2,1,0:T(4,128)S(1)} all-to-all(f32[32,4,128]{2,1,0:T(4,128)S(1)} %broadcast_in_dim.27), channel_id=1, replica_groups=mesh['row'=4,'col'=8] {'row','col'}, dimensions={0} | all-to-all | bytes 131072 | tf_op jit(solution)/shard_map/all_to_all | solution.py:322
  298.0 2.6 all-to-all-start.13
  301.9 4.7 %collective-permute-start.8 = (f32[64,128]{1,0:T(8,128)S(1)}, f32[64,128]{1,0:T(8,128)S(1)}, u32[]{:S(2)}, u32[]{:S(2)}) collective-permute-start(f32[64,128]{1,0:T(8,128)S(1)} %get-tuple-element.84), channel_id=1, source_target_pairs={{0,1},{1,2},{2,3},{3,4},{4,5},{5,6},{6,7},{7,8},{8,9},{9,10},{10,1... | collective-permute-start | bytes 98312 | tf_op jit(solution)/shard_map/ppermute | solution.py:327
  306.6 1.4 collective-permute-done.8.refs_8_
  308.0 3.2 all-to-all-done.13.refs_7_
  311.2 2.2 copy-done.5
  313.4 2.2 copy-done.12
  315.6 1.4 copy-done.19
  317.0 13.4 %advance.10 = (f32[192,2048]{1,0:T(8,128)S(1)}, f32[128,256]{1,0:T(8,128)S(1)}, f32[32,128]{1,0:T(8,128)S(1)}, f32[128,128]{1,0:T(8,128)S(1)}, f32[64,128]{1,0:T...) custom-call(s32[16,4]{1,0:T(8,128)S(1)} %copy.17.refs_0_, f32[2]{0:T(128)S(1)} %copy-done.24, ...), custom_call_target="tpu_custom_call" | custom-call | tf_op jit(solution)/shard_map/advance/pallas_call | solution.py:279
  330.4 13.3 %all_to_all.103 = f32[32,4,128]{2,1,0:T(4,128)S(1)} all-to-all(f32[32,4,128]{2,1,0:T(4,128)S(1)} %bitcast.52), channel_id=1, replica_groups=mesh['row'=4,'col'=8] {'row','col'}, dimensions={0} | all-to-all | bytes 131072 | tf_op jit(solution)/shard_map/all_to_all | solution.py:322
  343.8 9.0 %all_to_all.104 = f32[32,4,128]{2,1,0:T(4,128)S(1)} all-to-all(f32[32,4,128]{2,1,0:T(4,128)S(1)} %broadcast_in_dim.56), channel_id=1, replica_groups=mesh['row'=4,'col'=8] {'row','col'}, dimensions={0} | all-to-all | bytes 131072 | tf_op jit(solution)/shard_map/all_to_all | solution.py:322
  352.7 2.6 all-to-all-start.16
  356.7 4.8 %collective-permute-start.10 = (f32[64,128]{1,0:T(8,128)S(1)}, f32[64,128]{1,0:T(8,128)S(1)}, u32[]{:S(2)}, u32[]{:S(2)}) collective-permute-start(f32[64,128]{1,0:T(8,128)S(1)} %get-tuple-element.91), channel_id=1, source_target_pairs={{0,1},{1,2},{2,3},{3,4},{4,5},{5,6},{6,7},{7,8},{8,9},{9,10},{10,1... | collective-permute-start | bytes 98312 | tf_op jit(solution)/shard_map/ppermute | solution.py:327
  362.8 3.2 all-to-all-done.16.refs_7_
  366.0 2.2 copy-done.6
  368.2 2.2 copy-done.13
  370.3 13.4 %advance.11 = (f32[192,2048]{1,0:T(8,128)S(1)}, f32[128,256]{1,0:T(8,128)}, f32[32,128]{1,0:T(8,128)}, f32[128,128]{1,0:T(8,128)}, f32[64,128]{1,0:T(8,128)}, /*...) custom-call(s32[16,4]{1,0:T(8,128)S(1)} %copy.17.refs_0_, f32[2]{0:T(128)S(1)} %copy-done.24, ...), custom_call_target="tpu_custom_call" | custom-call | tf_op jit(solution)/shard_map/advance/pallas_call | solution.py:279
  384.9 6.3 %all-to-all-start.17 = ((f32[32,4,128]{2,1,0:T(4,128)}), f32[32,4,128]{2,1,0:T(4,128)S(1)}, u32[]{:S(2)}, u32[]{:S(2)}) async-start(f32[32,4,128]{2,1,0:T(4,128)} %bitcast.21), calls=%async_computation.17 | async-start | bytes 131072 | tf_op jit(solution)/shard_map/all_to_all | solution.py:322
  391.8 6.6 %all-to-all-done.17 = f32[32,4,128]{2,1,0:T(4,128)S(1)} async-done(((f32[32,4,128]{2,1,0:T(4,128)}), f32[32,4,128]{2,1,0:T(4,128)S(1)}, u32[]{:S(2)}, u32[]{:S(2)}) %all-to-all-start.17) | async-done | bytes 65568 | tf_op jit(solution)/shard_map/all_to_all | solution.py:322
  399.1 2.6 all-to-all-start.18
  402.4 6.6 %all-to-all-done.18 = f32[32,4,128]{2,1,0:T(4,128)S(1)} async-done(((f32[32,4,128]{2,1,0:T(4,128)}), f32[32,4,128]{2,1,0:T(4,128)S(1)}, u32[]{:S(2)}, u32[]{:S(2)}) %all-to-all-start.18) | async-done | bytes 65568 | tf_op jit(solution)/shard_map/all_to_all | solution.py:322
  409.0 1.4 copy-done.23
  410.4 8.2 %finish.1 = (f32[64,2048]{1,0:T(8,128)}, f32[3,64,64]{2,1,0:T(8,128)S(1)}) custom-call(f32[128,128]{1,0:T(8,128)S(1)} %bitcast.48, f32[64,128]{1,0:T(8,128)S(1)} %get-tuple-element.93.inner, f32[192,2048]{1,0:T(8,128)S(1)} %copy-done.23), custom_call_target="tpu_custom_call" | custom-call | tf_op jit(solution)/shard_map/finish/pallas_call | solution.py:297
  (78 shorter events, 20.7 us)
Async XLA Ops:
  3.8 55.6 %copy-start.15 = (f32[64,2048]{1,0:T(8,128)S(1)}, f32[64,2048]{1,0:T(8,128)}, u32[]{:S(2)}) copy-start(f32[64,2048]{1,0:T(8,128)} %refs_2_.1) | copy-start | bytes 1572868
  3.8 55.6 %copy-start.25 = (s32[1024]{0:T(1024)S(1)}, s32[1024]{0:T(1024)}, u32[]{:S(2)}) copy-start(s32[1024]{0:T(1024)} %param.12) | copy-start | bytes 12292
  3.8 55.6 %all-to-all-start = ((bf16[8,128,1024]{2,1,0:T(8,128)(2,1)}), bf16[8,128,1024]{2,1,0:T(8,128)(2,1)S(1)}, u32[]{:S(2)}, u32[]{:S(2)}) async-start(bf16[8,128,1024]{2,1,0:T(8,128)(2,1)} %bitcast.56), calls=%async_computation | async-start | bytes 4194304 | tf_op jit(solution)/shard_map/all_to_all | solution.py:338
  11.2 68.7 %copy-start.24 = (f32[2]{0:T(128)S(1)}, f32[2]{0:T(128)}, u32[]{:S(2)}) copy-start(f32[2]{0:T(128)} %refs_1_.11) | copy-start | bytes 28
  11.2 68.7 %copy-start.26 = (s32[128]{0:T(128)S(1)}, s32[128]{0:T(128)}, u32[]{:S(2)}) copy-start(s32[128]{0:T(128)} %param.11) | copy-start | bytes 1540
  74.1 2.0 copy-start
  76.1 19.9 %all-to-all-start.1 = ((f32[32,16,128]{2,1,0:T(8,128)}), f32[32,16,128]{2,1,0:T(8,128)S(1)}, u32[]{:S(2)}, u32[]{:S(2)}) async-start(f32[32,16,128]{2,1,0:T(8,128)} %bitcast.3), calls=%async_computation.1 | async-start | bytes 524288 | tf_op jit(solution)/shard_map/all_to_all | solution.py:322
  79.9 2.8 copy-start.14
  82.7 11.7 %copy-start.28 = (s32[16,4]{0,1:T(4,128)S(1)}, s32[16,4]{0,1:T(4,128)}, u32[]{:S(2)}) copy-start(s32[16,4]{0,1:T(4,128)} %param.10) | copy-start | bytes 772
  86.6 2.0 copy-start.7
  88.6 5.9 %collective-permute-start.1 = (f32[64,128]{1,0:T(8,128)S(1)}, f32[64,128]{1,0:T(8,128)S(1)}, u32[]{:S(2)}, u32[]{:S(2)}) collective-permute-start(f32[64,128]{1,0:T(8,128)S(1)} %get-tuple-element.53), channel_id=1, source_target_pairs={{1,0},{2,1},{3,2},{4,3},{5,4},{6,5},{7,6},{8,7},{9,8},{10,9},{11,1... | collective-permute-start | bytes 98312 | tf_op jit(solution)/shard_map/ppermute | solution.py:327
  89.9 6.1 %collective-permute-start = (f32[64,128]{1,0:T(8,128)S(1)}, f32[64,128]{1,0:T(8,128)S(1)}, u32[]{:S(2)}, u32[]{:S(2)}) collective-permute-start(f32[64,128]{1,0:T(8,128)S(1)} %get-tuple-element.53), channel_id=1, source_target_pairs={{0,1},{1,2},{2,3},{3,4},{4,5},{5,6},{6,7},{7,8},{8,9},{9,10},{10,1... | collective-permute-start | bytes 98312 | tf_op jit(solution)/shard_map/ppermute | solution.py:327
  96.0 2.2 copy-start.1
  98.2 2.2 copy-start.8
  106.2 1.1 copy-start.20
  132.9 13.2 %all-to-all-start.4 = ((f32[32,16,128]{2,1,0:T(8,128)}), f32[32,16,128]{2,1,0:T(8,128)S(1)}, u32[]{:S(2)}, u32[]{:S(2)}) async-start(f32[32,16,128]{2,1,0:T(8,128)} %bitcast.8), calls=%async_computation.4 | async-start | bytes 524288 | tf_op jit(solution)/shard_map/all_to_all | solution.py:322
  135.5 6.1 %collective-permute-start.3 = (f32[64,128]{1,0:T(8,128)S(1)}, f32[64,128]{1,0:T(8,128)S(1)}, u32[]{:S(2)}, u32[]{:S(2)}) collective-permute-start(f32[64,128]{1,0:T(8,128)S(1)} %get-tuple-element.63), channel_id=1, source_target_pairs={{1,0},{2,1},{3,2},{4,3},{5,4},{6,5},{7,6},{8,7},{9,8},{10,9},{11,1... | collective-permute-start | bytes 98312 | tf_op jit(solution)/shard_map/ppermute | solution.py:327
  136.8 6.1 %collective-permute-start.2 = (f32[64,128]{1,0:T(8,128)S(1)}, f32[64,128]{1,0:T(8,128)S(1)}, u32[]{:S(2)}, u32[]{:S(2)}) collective-permute-start(f32[64,128]{1,0:T(8,128)S(1)} %get-tuple-element.63), channel_id=1, source_target_pairs={{0,1},{1,2},{2,3},{3,4},{4,5},{5,6},{6,7},{7,8},{8,9},{9,10},{10,1... | collective-permute-start | bytes 98312 | tf_op jit(solution)/shard_map/ppermute | solution.py:327
  146.1 2.2 copy-start.2
  148.3 2.2 copy-start.9
  150.5 1.4 copy-start.21
  187.6 13.2 %all-to-all-start.7 = ((f32[32,16,128]{2,1,0:T(8,128)}), f32[32,16,128]{2,1,0:T(8,128)S(1)}, u32[]{:S(2)}, u32[]{:S(2)}) async-start(f32[32,16,128]{2,1,0:T(8,128)} %bitcast.11), calls=%async_computation.7 | async-start | bytes 524288 | tf_op jit(solution)/shard_map/all_to_all | solution.py:322
  190.2 6.1 %collective-permute-start.5 = (f32[64,128]{1,0:T(8,128)S(1)}, f32[64,128]{1,0:T(8,128)S(1)}, u32[]{:S(2)}, u32[]{:S(2)}) collective-permute-start(f32[64,128]{1,0:T(8,128)S(1)} %get-tuple-element.70), channel_id=1, source_target_pairs={{1,0},{2,1},{3,2},{4,3},{5,4},{6,5},{7,6},{8,7},{9,8},{10,9},{11,1... | collective-permute-start | bytes 98312 | tf_op jit(solution)/shard_map/ppermute | solution.py:327
  191.5 6.1 %collective-permute-start.4 = (f32[64,128]{1,0:T(8,128)S(1)}, f32[64,128]{1,0:T(8,128)S(1)}, u32[]{:S(2)}, u32[]{:S(2)}) collective-permute-start(f32[64,128]{1,0:T(8,128)S(1)} %get-tuple-element.70), channel_id=1, source_target_pairs={{0,1},{1,2},{2,3},{3,4},{4,5},{5,6},{6,7},{7,8},{8,9},{9,10},{10,1... | collective-permute-start | bytes 98312 | tf_op jit(solution)/shard_map/ppermute | solution.py:327
  200.8 2.2 copy-start.3
  203.0 2.2 copy-start.10
  218.6 1.1 copy-start.16
  242.1 13.2 %all-to-all-start.10 = ((f32[32,16,128]{2,1,0:T(8,128)}), f32[32,16,128]{2,1,0:T(8,128)S(1)}, u32[]{:S(2)}, u32[]{:S(2)}) async-start(f32[32,16,128]{2,1,0:T(8,128)} %bitcast.14), calls=%async_computation.10 | async-start | bytes 524288 | tf_op jit(solution)/shard_map/all_to_all | solution.py:322
  244.7 6.3 %collective-permute-start.7 = (f32[64,128]{1,0:T(8,128)S(1)}, f32[64,128]{1,0:T(8,128)S(1)}, u32[]{:S(2)}, u32[]{:S(2)}) collective-permute-start(f32[64,128]{1,0:T(8,128)S(1)} %get-tuple-element.77), channel_id=1, source_target_pairs={{1,0},{2,1},{3,2},{4,3},{5,4},{6,5},{7,6},{8,7},{9,8},{10,9},{11,1... | collective-permute-start | bytes 98312 | tf_op jit(solution)/shard_map/ppermute | solution.py:327
  246.0 6.1 %collective-permute-start.6 = (f32[64,128]{1,0:T(8,128)S(1)}, f32[64,128]{1,0:T(8,128)S(1)}, u32[]{:S(2)}, u32[]{:S(2)}) collective-permute-start(f32[64,128]{1,0:T(8,128)S(1)} %get-tuple-element.77), channel_id=1, source_target_pairs={{0,1},{1,2},{2,3},{3,4},{4,5},{5,6},{6,7},{7,8},{8,9},{9,10},{10,1... | collective-permute-start | bytes 98312 | tf_op jit(solution)/shard_map/ppermute | solution.py:327
  255.3 2.2 copy-start.4
  257.5 2.2 copy-start.11
  259.7 1.4 copy-start.17
  274.5 1.1 copy-start.18
  298.0 13.2 %all-to-all-start.13 = ((f32[32,16,128]{2,1,0:T(8,128)}), f32[32,16,128]{2,1,0:T(8,128)S(1)}, u32[]{:S(2)}, u32[]{:S(2)}) async-start(f32[32,16,128]{2,1,0:T(8,128)} %bitcast.17), calls=%async_computation.13 | async-start | bytes 524288 | tf_op jit(solution)/shard_map/all_to_all | solution.py:322
  300.6 6.1 %collective-permute-start.9 = (f32[64,128]{1,0:T(8,128)S(1)}, f32[64,128]{1,0:T(8,128)S(1)}, u32[]{:S(2)}, u32[]{:S(2)}) collective-permute-start(f32[64,128]{1,0:T(8,128)S(1)} %get-tuple-element.84), channel_id=1, source_target_pairs={{1,0},{2,1},{3,2},{4,3},{5,4},{6,5},{7,6},{8,7},{9,8},{10,9},{11,1... | collective-permute-start | bytes 98312 | tf_op jit(solution)/shard_map/ppermute | solution.py:327
  301.9 6.1 %collective-permute-start.8 = (f32[64,128]{1,0:T(8,128)S(1)}, f32[64,128]{1,0:T(8,128)S(1)}, u32[]{:S(2)}, u32[]{:S(2)}) collective-permute-start(f32[64,128]{1,0:T(8,128)S(1)} %get-tuple-element.84), channel_id=1, source_target_pairs={{0,1},{1,2},{2,3},{3,4},{4,5},{5,6},{6,7},{7,8},{8,9},{9,10},{10,1... | collective-permute-start | bytes 98312 | tf_op jit(solution)/shard_map/ppermute | solution.py:327
  311.2 2.2 copy-start.5
  313.4 2.2 copy-start.12
  315.6 1.4 copy-start.19
  352.7 13.2 %all-to-all-start.16 = ((f32[32,16,128]{2,1,0:T(8,128)}), f32[32,16,128]{2,1,0:T(8,128)S(1)}, u32[]{:S(2)}, u32[]{:S(2)}) async-start(f32[32,16,128]{2,1,0:T(8,128)} %bitcast.20), calls=%async_computation.16 | async-start | bytes 524288 | tf_op jit(solution)/shard_map/all_to_all | solution.py:322
  355.4 6.1 %collective-permute-start.11 = (f32[64,128]{1,0:T(8,128)S(1)}, f32[64,128]{1,0:T(8,128)S(1)}, u32[]{:S(2)}, u32[]{:S(2)}) collective-permute-start(f32[64,128]{1,0:T(8,128)S(1)} %get-tuple-element.91), channel_id=1, source_target_pairs={{1,0},{2,1},{3,2},{4,3},{5,4},{6,5},{7,6},{8,7},{9,8},{10,9},{11,1... | collective-permute-start | bytes 98312 | tf_op jit(solution)/shard_map/ppermute | solution.py:327
  356.7 6.1 %collective-permute-start.10 = (f32[64,128]{1,0:T(8,128)S(1)}, f32[64,128]{1,0:T(8,128)S(1)}, u32[]{:S(2)}, u32[]{:S(2)}) collective-permute-start(f32[64,128]{1,0:T(8,128)S(1)} %get-tuple-element.91), channel_id=1, source_target_pairs={{0,1},{1,2},{2,3},{3,4},{4,5},{5,6},{6,7},{7,8},{8,9},{9,10},{10,1... | collective-permute-start | bytes 98312 | tf_op jit(solution)/shard_map/ppermute | solution.py:327
  361.4 0.8 copy-start.27
  366.0 2.2 copy-start.6
  368.2 2.2 copy-start.13
  383.7 1.2 copy-start.22
  384.9 13.5 %all-to-all-start.17 = ((f32[32,4,128]{2,1,0:T(4,128)}), f32[32,4,128]{2,1,0:T(4,128)S(1)}, u32[]{:S(2)}, u32[]{:S(2)}) async-start(f32[32,4,128]{2,1,0:T(4,128)} %bitcast.21), calls=%async_computation.17 | async-start | bytes 131072 | tf_op jit(solution)/shard_map/all_to_all | solution.py:322
  399.1 9.9 %all-to-all-start.18 = ((f32[32,4,128]{2,1,0:T(4,128)}), f32[32,4,128]{2,1,0:T(4,128)S(1)}, u32[]{:S(2)}, u32[]{:S(2)}) async-start(f32[32,4,128]{2,1,0:T(4,128)} %broadcast_in_dim.57), calls=%async_computation.18 | async-start | bytes 131072 | tf_op jit(solution)/shard_map/all_to_all | solution.py:322
  409.0 1.4 copy-start.23

commit v2 on v1

v2 whole, which is shorter than its diff:
```python
import functools

import jax
import jax.numpy as jnp
from jax import lax
from jax.experimental import pallas as pl
from jax.experimental.pallas import tpu as pltpu
from jax.sharding import PartitionSpec as P

STEPS = 6
AXES = ("row", "col")
VMEM = pl.BlockSpec(memory_space=pltpu.VMEM)
SMEM = pl.BlockSpec(memory_space=pltpu.SMEM)
HBM = pl.BlockSpec(memory_space=pltpu.HBM)
F32 = jnp.float32
BF16 = jnp.bfloat16
LIMIT = 40 * 1024 * 1024


def exact(left, right):
    return lax.dot_general(
        left, right, (((1,), (0,)), ((), ())), precision=lax.Precision.HIGHEST, preferred_element_type=F32
    )


def exact_rows(left, right):
    return lax.dot_general(
        left, right, (((1,), (1,)), ((), ())), precision=lax.Precision.HIGHEST, preferred_element_type=F32
    )


def rows(left, right):
    return lax.dot_general(left, right, (((1,), (1,)), ((), ())), preferred_element_type=F32)


def combine_kernel(rates, rim, wet, start, blocks, mixed, pick, place, halo):
    size = blocks.shape[-1]
    for k in range(blocks.shape[2]):
        whole = (
            blocks[0, 0, k].astype(F32)
            + rates[0] * blocks[1, 0, k].astype(F32)
            - rates[1] * blocks[2, 0, k].astype(F32)
        ).T
        high = whole.astype(BF16)
        mixed[0, k * size : (k + 1) * size, :size] = high
        mixed[0, k * size : (k + 1) * size, size:] = (whole - high.astype(F32)).astype(BF16)

    @pl.when(pl.program_id(0) == 0)
    def _():
        index = lax.broadcasted_iota(jnp.int32, pick.shape, 0)
        pick[...] = jnp.where(index == rim[...], 1.0, 0.0).astype(BF16)
        index = lax.broadcasted_iota(jnp.int32, place.shape, 1)
        place[...] = jnp.where(index == wet[...], 1.0, 0.0).astype(BF16)
        halo[...] = jnp.dot(start[...].astype(BF16), pick[...], preferred_element_type=F32)


def combine(rates, rim, wet, start, blocks):
    _, count, nnz, size, _ = blocks.shape
    vectors, width = start.shape
    whole = lambda shape: pl.BlockSpec(shape, lambda i: (0,) * len(shape))
    return pl.pallas_call(
        combine_kernel,
        grid=(count,),
        in_specs=[
            SMEM,
            whole(rim.shape),
            whole(wet.shape),
            whole(start.shape),
            pl.BlockSpec((3, 1, nnz, size, size), lambda i: (0, i, 0, 0, 0)),
        ],
        out_specs=[
            pl.BlockSpec((1, nnz * size, 2 * size), lambda i: (i, 0, 0)),
            whole((width, rim.shape[1])),
            whole((wet.shape[0], width)),
            whole((vectors, rim.shape[1])),
        ],
        out_shape=[
            jax.ShapeDtypeStruct((count, nnz * size, 2 * size), BF16),
            jax.ShapeDtypeStruct((width, rim.shape[1]), BF16),
            jax.ShapeDtypeStruct((wet.shape[0], width), BF16),
            jax.ShapeDtypeStruct((vectors, rim.shape[1]), F32),
        ],
        compiler_params=pltpu.CompilerParams(vmem_limit_bytes=LIMIT),
        name="combine",
    )(rates, rim, wet, start, blocks)


def spread_kernel(count, slots, start, mass, spread, part, own, total):
    n_col, n_row, _, half, wcap = mass.shape
    size = n_col * half
    step = pl.program_id(0)

    @pl.when(step == 0)
    def _():
        for h in range(2):
            for r in range(n_row):
                first = (h * n_row + r) * size
                own[first : first + size] = mass[:, r, h].reshape(size, wcap)
        total[...] = jnp.zeros_like(total)

    slot = lax.broadcasted_iota(jnp.int32, slots.shape, 1)
    live = jnp.where(slot < count[0], slots[...], -1)
    columns, vectors = spread.shape[1], start.shape[0]
    index = lax.broadcasted_iota(jnp.int32, (columns, wcap), 0) + step * columns
    onehot = jnp.where(index == live, 1.0, 0.0).astype(BF16)
    block = rows(own[...], onehot).astype(BF16)
    spread[...] = block
    total[...] += rows(block, start[...].astype(BF16))

    @pl.when(step == pl.num_programs(0) - 1)
    def _():
        part[:, :vectors] = total[: n_row * size]
        part[:, vectors:] = total[n_row * size :]


def spread_mass(count, slots, start, mass):
    n_col, n_row, _, half, wcap = mass.shape
    vectors, width = start.shape
    size = n_col * n_row * half
    columns = min(width, 512)
    return pl.pallas_call(
        spread_kernel,
        grid=(width // columns,),
        in_specs=[
            SMEM,
            pl.BlockSpec(slots.shape, lambda i: (0, 0)),
            pl.BlockSpec((vectors, columns), lambda i: (0, i)),
            pl.BlockSpec(mass.shape, lambda i: (0,) * 5),
        ],
        out_specs=[
            pl.BlockSpec((2 * size, columns), lambda i: (0, i)),
            pl.BlockSpec((size, 2 * vectors), lambda i: (0, 0)),
        ],
        out_shape=[
            jax.ShapeDtypeStruct((2 * size, width), BF16),
            jax.ShapeDtypeStruct((size, 2 * vectors), F32),
        ],
        scratch_shapes=[pltpu.VMEM((2 * size, wcap), BF16), pltpu.VMEM((2 * size, vectors), F32)],
        compiler_params=pltpu.CompilerParams(vmem_limit_bytes=LIMIT),
        name="spread",
    )(count, slots, start, mass)


def coefficients_of(total, gram, inner, mix, coef):
    n = gram.shape[0] // 2
    scale = 1.0 / total
    aa = gram[:n, :n] * scale
    self_ = gram[:n, n:] * scale
    prev = gram[n:, :n] * scale
    cc = gram[n:, n:] * scale
    cp = inner[:, :n]
    pp = inner[:, n:]
    mix[:, :n] = -self_
    mix[:, n:] = -prev
    coef[0] = self_
    coef[1] = prev
    t_c = self_ - exact(self_, cc) - exact_rows(prev, cp)
    t_p = prev - exact(self_, cp) - exact(prev, pp)
    t_a = aa - exact_rows(self_, self_) - exact_rows(prev, prev)
    matrix = t_a - exact_rows(t_c, self_) - exact_rows(t_p, prev)
    return 0.5 * (matrix + matrix.T), t_c, cc


def eliminate(matrix, beside, coef, factor_t):
    n = matrix.shape[0]
    row_id = lax.broadcasted_iota(jnp.int32, (n, 2 * n), 0)
    lane_id = lax.broadcasted_iota(jnp.int32, (n, 2 * n), 1)
    factor_t[...] = jnp.where(row_id + n == lane_id, 1.0, 0.0)
    factor_t[:, :n] = matrix
    work = [factor_t[g * 8 : (g + 1) * 8, :] for g in range(n // 8)]
    sub = lax.broadcasted_iota(jnp.int32, (8, 1), 0)
    done = 0
    for j in range(0, n, 2):
        g, s = divmod(j, 8)
        top = work[g][s : s + 1, :]
        low = work[g][s + 1 : s + 2, :]
        a, b, c = top[:, j : j + 1], top[:, j + 1 : j + 2], low[:, j + 1 : j + 2]
        scale = 1.0 / (a * c - b * b)
        new_top = (c * top - b * low) * scale
        new_low = (a * low - b * top) * scale
        for i in range(g, n // 8):
            left, right = work[i][:, j : j + 1], work[i][:, j + 1 : j + 2]
            if i == g:
                left = jnp.where(sub > s + 1, left, 0.0)
                right = jnp.where(sub > s + 1, right, 0.0)
            work[i] = work[i] - (left * new_top + right * new_low)
        goal = len(beside) * (j + 2) // n
        while done < goal:
            beside[done]()
            done += 1
    reduced = jnp.concatenate(work, 0)
    above = pltpu.roll(reduced, 1, 0)
    odd = lax.broadcasted_iota(jnp.int32, (n, 1), 0) % 2 == 1
    pick = lambda values, where: jnp.sum(jnp.where(where, values, 0.0), 1, keepdims=True)
    under = pick(above, lane_id == row_id) / jnp.where(odd, pick(above, lane_id + 1 == row_id), 1.0)
    reduced = reduced - jnp.where(odd, under, 0.0) * above
    diagonal = pick(reduced, lane_id == row_id)
    scale = lax.rsqrt(diagonal)
    scale = scale * (1.5 - 0.5 * diagonal * scale * scale)
    reduced = reduced * scale
    factor_t[...] = reduced
    upper = jnp.where(row_id <= lane_id, reduced, 0.0)
    coef[2] = upper.T[:n, :]
    return factor_t[:, n:]


def thirds(values):
    high = values.astype(BF16)
    rest = values - high.astype(F32)
    middle = rest.astype(BF16)
    return jnp.concatenate([high, middle, (rest - middle.astype(F32)).astype(BF16)], 0)


def unpack(lines, received, target, lanes, offset):
    for s in range(received.shape[0]):
        if s * lines < target.shape[0]:
            target[s * lines : (s + 1) * lines, lanes] = received[s, offset : offset + lines]


def advance_kernel(mode, total, peers, *refs):
    it = iter(refs)
    take = lambda k: [next(it) for _ in range(k)]
    ids, rates = take(2)
    if mode == "first":
        arrived, below, above, held_in = take(4)
        held = [held_in]
    else:
        received, pressed, inner, edges, wet_held = take(5)
        held = take(3)
    pick, place, mixed_in, spread_in = take(4)
    (applied_out,) = take(1)
    edges_out, wet_out, send = take(3) if mode != "last" else (None, None, None)
    if mode == "last":
        (gram_s,) = take(1)
    if mode != "first":
        current_out, inner_out, coef = take(3)
    extended, split, stack, fresh, mixed, spread, sems = take(7)
    if mode != "last":
        (gram_s,) = take(1)
    if mode != "first":
        factor_t, mix, gram_in, edge_in = take(4)
    else:
        (edge_in,) = take(1)

    n = fresh.shape[0]
    width = fresh.shape[1] // 2
    size = edge_in.shape[1] // 2
    count = width // size
    glines = -(-2 * n // peers)
    hlines = -(-n // peers)
    loads = []
    for k, source in enumerate(held):
        place_at = stack.at[pl.ds(k * n, n)] if mode != "first" else fresh.at[:, pl.ds(width, width)]
        loads.append(pltpu.make_async_copy(source, place_at, sems.at[k]))
    load_mixed = pltpu.make_async_copy(mixed_in, mixed, sems.at[3])
    for copy in loads + [load_mixed]:
        copy.start()
    if mode != "last":
        load_spread = pltpu.make_async_copy(spread_in, spread, sems.at[4])
        load_spread.start()

    if mode == "first":
        edge_in[:n, :size] = below[...]
        edge_in[:n, size:] = above[...]
        summed = jnp.sum(arrived[...], 0)
    else:
        unpack(glines, received, gram_in, slice(None), 0)
        unpack(hlines, received, edge_in.at[pl.ds(0, n)], slice(0, size), glines)
        unpack(hlines, received, edge_in.at[pl.ds(0, n)], slice(size, 2 * size), glines + hlines)
        edge_in[n:, :] = edges[...]
        summed = pressed[...]
        matrix, t_c, cc = coefficients_of(total, gram_in, inner, mix, coef)
    wet = jnp.concatenate([summed[:, :n], summed[:, n:]], 0)
    edge = edge_in[:n, :]
    for copy in loads:
        copy.wait()
    if mode == "first":
        residual = fresh[:, width:]
    else:
        wet = wet + exact_rows(wet_held[...], mix[...])
        edge = edge + exact(mix[...], edge_in[n:, :])
        residual = stack[:n, :] + exact(mix[...], stack[n:, :])
        stack[:n, :] = residual
    for i in range(count):
        extended[i] = residual[:, i * size : (i + 1) * size].astype(BF16)
    extended[count] = edge[:, :size].astype(BF16)
    extended[count + 1] = edge[:, size:].astype(BF16)
    force = thirds(wet.T * rates[1])
    load_mixed.wait()

    def block(i):
        picked = jnp.concatenate([extended[ids[i, k]] for k in range(ids.shape[1])], 1)
        both = jnp.dot(picked, mixed[i], preferred_element_type=F32)
        lanes = slice(i * size, (i + 1) * size)
        added = jnp.dot(force, place[:, lanes], preferred_element_type=F32)
        fresh[:, lanes] = both[:, :size] + both[:, size:] - (added[:n] + added[n : 2 * n] + added[2 * n :])

    beside = [functools.partial(block, i) for i in range(count)]
    stores = []
    if mode == "first":
        for emit in beside:
            emit()
        edges_out[:n, :] = edge
        edges_out[n:, :] = jnp.zeros_like(edge)
        wet_out[:, :n] = wet
        wet_out[:, n:] = jnp.zeros_like(wet)
    else:
        inverse = eliminate(matrix, beside, coef, factor_t)
        fresh[:, width:] = exact(inverse, stack[:n, :])
        stores.append(pltpu.make_async_copy(fresh.at[:, pl.ds(width, width)], current_out, sems.at[5]))
        stores[-1].start()
        fresh[:, :width] = exact(inverse, fresh[:, :width])
        inner_out[:, :n] = exact(inverse, t_c)
        inner_out[:, n:] = cc
        if mode != "last":
            edges_out[:n, :] = exact(inverse, edge)
            edges_out[n:, :] = edges[:n, :]
            wet_out[:, :n] = exact_rows(wet, inverse)
            wet_out[:, n:] = wet_held[:, :n]
    stores.append(pltpu.make_async_copy(fresh.at[:, pl.ds(0, width)], applied_out, sems.at[6]))
    stores[-1].start()
    applied = fresh[:, :width]
    current = fresh[:, width:]
    gram_s[:n, :n] = exact_rows(applied, applied)
    gram_s[:n, n:] = exact_rows(applied, current)
    if mode == "first":
        gram_s[n:, :n] = jnp.zeros((n, n), F32)
    else:
        gram_s[n : 2 * n, :n] = exact_rows(applied, stack[n : 2 * n, :])
    gram_s[n : 2 * n, n:] = exact_rows(current, current)
    if mode != "last":
        high = applied.astype(BF16)
        split[:n, :] = high
        split[n:, :] = (applied - high.astype(F32)).astype(BF16)
        rim = jnp.dot(split[...], pick[...], preferred_element_type=F32)
        edge_in[:n, :size] = rim[:n] + rim[n:]
        load_spread.wait()
        wets = wet_out.shape[0] // 2
        middle = spread.shape[0] // 2
        tops = rows(spread[:middle], split[...])
        tops = tops + pltpu.roll(tops, n, 1)
        ends = rows(spread[middle:], split[...])
        ends = ends + pltpu.roll(ends, n, 1)
        lane = lax.broadcasted_iota(jnp.int32, tops.shape, 1)
        send[:, :wets, :] = jnp.where(lane < n, tops, ends).reshape(peers, wets, 2 * n)
        rest = send.shape[1] - wets
        send[:, wets:, :] = jnp.zeros((peers, rest, 2 * n), F32)
        for d in range(peers):
            if d * glines < 2 * n:
                send[d, wets : wets + glines] = gram_s[d * glines : (d + 1) * glines, :]
            if d * hlines < n:
                send[d, wets + glines : wets + glines + hlines] = edge_in[d * hlines : (d + 1) * hlines, :size]
    for copy in stores:
        copy.wait()


def advance(mode, total, peers, ids, rates, state, fixed):
    mixed, pick, place, spread = fixed
    vectors, size = mixed.shape[1] // ids.shape[1] // 2, mixed.shape[2] // 2
    width = pick.shape[0]
    wets = place.shape[0]
    vectors = state[-1].shape[0]
    lines = -(-(wets // 2 + -(-2 * vectors // peers) + -(-vectors // peers)) // 8) * 8
    sds = jax.ShapeDtypeStruct
    block = sds((vectors, width), F32)
    shapes, specs = [block], [HBM]
    if mode != "last":
        shapes += [
            sds((2 * vectors, 2 * size), F32),
            sds((wets, 2 * vectors), F32),
            sds((peers, lines, 2 * vectors), F32),
        ]
        specs += [VMEM] * 3
    else:
        shapes += [sds((2 * vectors, 2 * vectors), F32)]
        specs += [VMEM]
    if mode != "first":
        shapes += [block, sds((vectors, 2 * vectors), F32), sds((3, vectors, vectors), F32)]
        specs += [HBM, VMEM, VMEM]
    scratch = [
        pltpu.VMEM((width // size + 2, vectors, size), BF16),
        pltpu.VMEM((2 * vectors, width), BF16),
        pltpu.VMEM((3 * vectors, width), F32),
        pltpu.VMEM((vectors, 2 * width), F32),
        pltpu.VMEM(mixed.shape, BF16),
        pltpu.VMEM(spread.shape, BF16),
        pltpu.SemaphoreType.DMA((7,)),
    ]
    if mode != "last":
        scratch += [pltpu.VMEM((2 * vectors, 2 * vectors), F32)]
    if mode != "first":
        scratch += [
            pltpu.VMEM((vectors, 2 * vectors), F32),
            pltpu.VMEM((vectors, 2 * vectors), F32),
            pltpu.VMEM((2 * vectors, 2 * vectors), F32),
            pltpu.VMEM((3 * vectors, 2 * size), F32),
        ]
        held = 3
    else:
        scratch += [pltpu.VMEM((vectors, 2 * size), F32)]
        held = 1
    return pl.pallas_call(
        functools.partial(advance_kernel, mode, total, peers),
        in_specs=[SMEM, SMEM] + [VMEM] * (len(state) - held) + [HBM] * held + [VMEM, VMEM, HBM, HBM],
        out_specs=specs,
        out_shape=shapes,
        scratch_shapes=scratch,
        compiler_params=pltpu.CompilerParams(vmem_limit_bytes=LIMIT),
        name="advance_" + mode,
    )(ids, rates, *state, pick, place, mixed, spread)


def route_kernel(vectors, wets, received, pressed, send):
    peers = received.shape[0]
    glines = -(-2 * vectors // peers)
    hlines = -(-vectors // peers)
    pressed[...] = jnp.sum(received[:, :wets, :], 0)
    mine = jnp.sum(received[:, wets:, :], 0)[:glines]
    edge = wets + glines
    nothing = jnp.zeros((hlines, 2 * vectors), F32)
    for t in range(peers):
        send[t] = jnp.zeros(send.shape[1:], F32)
        send[t, :glines] = mine
        send[t, glines : glines + hlines] = received[t - 1, edge : edge + hlines] if t > 0 else nothing
        send[t, glines + hlines : glines + 2 * hlines] = (
            received[t + 1, edge : edge + hlines] if t < peers - 1 else nothing
        )


def route(vectors, wets, received):
    peers = received.shape[0]
    return pl.pallas_call(
        functools.partial(route_kernel, vectors, wets),
        in_specs=[VMEM],
        out_specs=[VMEM] * 2,
        out_shape=[
            jax.ShapeDtypeStruct((wets, 2 * vectors), F32),
            jax.ShapeDtypeStruct((peers, 8, 2 * vectors), F32),
        ],
        compiler_params=pltpu.CompilerParams(vmem_limit_bytes=LIMIT),
        name="route",
    )(received)


def finish_kernel(total, gram_in, inner, applied, current, previous, out, coef, factor_t, mix, stack, sems):
    n = inner.shape[0]
    loads = []
    for k, source in enumerate((applied, current, previous)):
        loads.append(pltpu.make_async_copy(source, stack.at[pl.ds(k * n, n)], sems.at[k]))
        loads[-1].start()
    matrix, _, _ = coefficients_of(total, gram_in, inner, mix, coef)
    for copy in loads:
        copy.wait()

    def residual():
        stack[:n, :] = stack[:n, :] + exact(mix[...], stack[n:, :])

    inverse = eliminate(matrix, [residual], coef, factor_t)
    out[...] = exact(inverse, stack[:n, :])


def finish(total, gram, inner, held):
    vectors, width = held[0].shape
    return pl.pallas_call(
        functools.partial(finish_kernel, total),
        in_specs=[VMEM] * 2 + [HBM] * 3,
        out_specs=[VMEM] * 2,
        out_shape=[
            jax.ShapeDtypeStruct((vectors, width), F32),
            jax.ShapeDtypeStruct((3, vectors, vectors), F32),
        ],
        scratch_shapes=[
            pltpu.VMEM((vectors, 2 * vectors), F32),
            pltpu.VMEM((vectors, 2 * vectors), F32),
            pltpu.VMEM((3 * vectors, width), F32),
            pltpu.SemaphoreType.DMA((3,)),
        ],
        compiler_params=pltpu.CompilerParams(vmem_limit_bytes=LIMIT),
        name="finish",
    )(gram, inner, *held)


def local(n_row, n_col, start_block, struct_blocks, block_ids, rim_rows, wet_slots, wet_counts, added_mass, rates):
    peers = n_row * n_col
    vectors, width = start_block.shape
    total = float(width * peers)
    wcap = wet_slots.shape[0]
    wets = added_mass.shape[0] // n_row

    def exchange(parts):
        return lax.all_to_all(parts, AXES, 0, 0, tiled=True)

    def neighbours(halo):
        up = [(i, i + 1) for i in range(peers - 1)]
        down = [(i + 1, i) for i in range(peers - 1)]
        return lax.ppermute(halo, AXES, up), lax.ppermute(halo, AXES, down)

    def summed(gram):
        lines = gram.shape[0] // peers
        mine = exchange(gram.reshape(peers, lines, -1)).sum(0)
        return exchange(jnp.broadcast_to(mine[None], (peers, *mine.shape))).reshape(gram.shape)

    blocks = added_mass.reshape(-1, n_col, wcap).transpose(1, 0, 2)
    mass = lax.all_to_all(blocks, "col", 0, 0, tiled=True)
    mass = mass.reshape(n_col, n_row, 2, wets // 2, wcap)
    mixed, pick, place, halo = combine(
        rates, rim_rows[None, :], wet_slots[:wets, None], start_block, struct_blocks
    )
    spread, part = spread_mass(wet_counts, wet_slots[None, :], start_block, mass)
    fixed = (mixed, pick, place, spread)
    below, above = neighbours(halo)
    arrived = exchange(part.reshape(peers, wets // 2, 2 * vectors))
    step = functools.partial(advance, total=total, peers=peers, ids=block_ids, rates=rates, fixed=fixed)
    applied, edges, wet_held, send = step("first", state=(arrived, below, above, start_block))
    inner = jnp.zeros((vectors, 2 * vectors), F32)
    current, previous = start_block, jnp.zeros_like(start_block)
    coefficients = []
    for number in range(1, STEPS):
        pressed, again = route(vectors, wets // 2, exchange(send))
        received = exchange(again)
        state = (received, pressed, inner, edges, wet_held, applied, current, previous)
        if number < STEPS - 1:
            applied, edges, wet_held, send, following, inner, coef = step("mid", state=state)
        else:
            applied, gram, following, inner, coef = step("last", state=state)
        coefficients.append(coef)
        previous, current = current, following
    final, coef = finish(total, summed(gram), inner, (applied, current, previous))
    coefficients.append(coef)
    return final, jnp.stack(coefficients)


def solution(mesh):
    return jax.shard_map(
        functools.partial(local, mesh.shape["row"], mesh.shape["col"]),
        mesh=mesh,
        in_specs=(
            P(None, AXES),
            P(None, AXES, None, None, None),
            P(AXES, None),
            P(AXES),
            P(AXES),
            P(AXES),
            P("col", "row"),
            P(),
        ),
        out_specs=(P(None, AXES), P()),
        check_vma=False,
    )
```

time: 428 us -> 342 us (0.80)
  starting transfers between devices: 69.2 us -> 26.8 us
  local copies, waits for them, and re-layouts: 50.1 us -> 25.4 us
  Pallas kernels: 99.5 us -> 88.8 us
  blocking collectives: 115 us -> 108 us
    ppermute x12 -> x2, starting transfers between devices: 36.3 us -> 4.95 us  [neighbours(): return (lax.ppermute(halo, AXES, up), lax.ppermute(halo, AXES, down))]
    unnamed x64 -> x38, local copies, waits for them, and re-layouts: 45.5 us -> 20.7 us
    all_to_all x8 -> x5, starting transfers between devices: 25.4 us -> 14.5 us  [exchange(): return lax.all_to_all(parts, AXES, 0, 0, tiled=True)]
    pallas_call x7 -> x12, Pallas kernels: 87.4 us -> 77.4 us  [the longest x6 68.8 us: advance(): pl.pallas_call(functools.partial(advance_kernel, mode, total, peers), in_...]
    all_to_all x10 -> x8, blocking collectives: 115 us -> 108 us  [exchange(): return lax.all_to_all(parts, AXES, 0, 0, tiled=True)]
    all_to_all x8 -> x5, waiting for transfers between devices: 29.3 us -> 32.6 us  [exchange(): return lax.all_to_all(parts, AXES, 0, 0, tiled=True)]
  transfers between devices with their start and end apart: 21 -> 8, of which waited for: 14 -> 7; matrix products, arithmetic and copies ran while one was open for 0% -> 1% of each run, Pallas kernels for 1% -> 1%
where the time goes in v2:
time: 342 us; the launch traced here: 335 us
  blocking collectives  108 us (32%)
  Pallas kernels  88.8 us (26%)
  waiting for transfers between devices  84.6 us (25%)
  starting transfers between devices  26.8 us (8%)
  local copies, waits for them, and re-layouts  25.4 us (7%)
    all_to_all x8, blocking collectives, exchange(): return lax.all_to_all(parts, AXES, 0, 0, tiled=True)  108 us
    pallas_call x6, Pallas kernels, advance(): pl.pallas_call(functools.partial(advance_kernel, mode, total, peers), in_...  68.8 us
    all_to_all x1, waiting for transfers between devices, local(): mass = lax.all_to_all(blocks, 'col', 0, 0, tiled=True)  47.6 us
    all_to_all x5, waiting for transfers between devices, exchange(): return lax.all_to_all(parts, AXES, 0, 0, tiled=True)  32.6 us
    unnamed x38, local copies, waits for them, and re-layouts  20.7 us
    all_to_all x5, starting transfers between devices, exchange(): return lax.all_to_all(parts, AXES, 0, 0, tiled=True)  14.5 us
    pallas_call x1, Pallas kernels, spread_mass(): pl.pallas_call(spread_kernel, grid=(width // columns,), in_specs=[SMEM, p...  7.68 us
    pallas_call x1, Pallas kernels, finish(): pl.pallas_call(functools.partial(finish_kernel, total), in_specs=[VMEM] *...  7.47 us
  transfers between devices with their start and end apart: 8, of which 7 were waited for; matrix products, arithmetic and copies ran while one was open for 1% of the time, Pallas kernels for 1%

profile of v2, /device:TPU:0, one launch (start us, length us, event | category | flops | bytes accessed | tf_op | source)
XLA Modules:
  0.0 335.5 jit_solution(13241464187882186795)
XLA Ops:
  0.6 0.0 copy-start.8
  0.6 0.0 copy-start.13
  0.6 3.2 copy.20
  3.9 7.4 %all-to-all-start = ((bf16[8,128,1024]{2,1,0:T(8,128)(2,1)}), bf16[8,128,1024]{2,1,0:T(8,128)(2,1)S(1)}, u32[]{:S(2)}, u32[]{:S(2)}) async-start(bf16[8,128,1024]{2,1,0:T(8,128)(2,1)} %bitcast.31), calls=%async_computation | async-start | bytes 4194304 | tf_op jit(solution)/shard_map/all_to_all | solution.py:504
  11.9 47.6 %all-to-all-done = bf16[8,128,1024]{2,1,0:T(8,128)(2,1)S(1)} async-done(((bf16[8,128,1024]{2,1,0:T(8,128)(2,1)}), bf16[8,128,1024]{2,1,0:T(8,128)(2,1)S(1)}, u32[]{:S(2)}, u32[]{:S(2)}) %all-to-all-start) | async-done | bytes 2097184 | tf_op jit(solution)/shard_map/all_to_all | solution.py:504
  59.5 0.0 copy-done.8
  59.5 0.0 copy-done.13
  59.5 7.7 %spread.1 = (bf16[1024,2048]{1,0:T(8,128)(2,1)S(1)}, f32[512,128]{1,0:T(8,128)}) custom-call(s32[1]{0:T(128)S(6)} %copy.26.count, s32[1,1024]{1,0:T(1,128)S(1)} %bitcast.29, f32[64,2048]{1,0:T(8,128)S(1)} %copy-done.8, bf16[8,4,2,16,1024]{4,3,2,1,0:T(8,128)(2,1)S(1)} %bitcast.27), custom_call_target="tpu_custom_call" | custom-call | tf_op jit(solution)/shard_map/spread/pallas_call | solution.py:121
  67.2 2.0 copy-done
  69.2 3.7 %all-to-all-start.1 = ((f32[32,16,128]{2,1,0:T(8,128)}), f32[32,16,128]{2,1,0:T(8,128)S(1)}, u32[]{:S(2)}, u32[]{:S(2)}) async-start(f32[32,16,128]{2,1,0:T(8,128)} %bitcast.3), calls=%async_computation.1 | async-start | bytes 524288 | tf_op jit(solution)/shard_map/all_to_all | solution.py:491
  72.9 0.1 copy.11.wet
  73.0 0.0 copy-done.12
  73.0 2.8 copy-done.9
  75.8 3.9 %combine.1 = (bf16[16,512,256]{2,1,0:T(8,128)(2,1)S(1)}, bf16[2048,128]{1,0:T(8,128)(2,1)S(1)}, bf16[32,2048]{1,0:T(8,128)(2,1)S(1)}, f32[64,128]{1,0:T(8,128)S(1)}) custom-call(f32[2]{0:T(128)S(1)} %copy-done.12, s32[1,128]{1,0:T(1,128)S(1)} %bitcast.30, s32[32,1]{1,0:T(8,128)S(1)} %copy.11.wet, f32[64,2048]{1,0:T(8,128)S(1)} %copy-done.8, ...), custom_call_target="tpu_custom_call" | custom-call | tf_op jit(solution)/shard_map/combine/pallas_call | solution.py:61
  79.8 0.0 copy-start.4
  79.8 2.0 copy-done.4
  81.7 3.7 %collective-permute-start = (f32[64,128]{1,0:T(8,128)S(1)}, f32[64,128]{1,0:T(8,128)S(1)}, u32[]{:S(2)}, u32[]{:S(2)}) collective-permute-start(f32[64,128]{1,0:T(8,128)S(1)} %get-tuple-element.58), channel_id=1, source_target_pairs={{0,1},{1,2},{2,3},{3,4},{4,5},{5,6},{6,7},{7,8},{8,9},{9,10},{10,1... | collective-permute-start | bytes 98312 | tf_op jit(solution)/shard_map/ppermute | solution.py:496
  85.4 1.3 collective-permute-start.1
  86.7 0.1 copy.17.refs_0_
  86.8 0.2 collective-permute-done.refs_3_
  87.0 4.2 %collective-permute-done.1.refs_4_ = f32[64,128]{1,0:T(8,128)S(1)} collective-permute-done((f32[64,128]{1,0:T(8,128)S(1)}, f32[64,128]{1,0:T(8,128)S(1)}, u32[]{:S(2)}, u32[]{:S(2)}) %collective-permute-start.1) | collective-permute-done | bytes 32800 | tf_op jit(solution)/shard_map/ppermute | solution.py:496
  91.2 0.0 all-to-all-done.1.refs_2_
  91.2 2.2 copy-done.1
  93.4 2.2 copy-done.5
  95.6 5.9 %advance_first.1 = (f32[64,2048]{1,0:T(8,128)S(1)}, f32[128,256]{1,0:T(8,128)S(1)}, f32[32,128]{1,0:T(8,128)S(1)}, f32[32,24,128]{2,1,0:T(8,128)S(1)}) custom-call(s32[16,4]{1,0:T(8,128)S(1)} %copy.17.refs_0_, f32[2]{0:T(128)S(1)} %copy-done.12, f32[32,16,128]{2,1,0:T(8,128)S(1)} %all-to-all-done.1.refs_2_, f32[64,128]{1,0:T(8,128)S(1)} %collective-permute-done.refs_3_, ...), custom_call_target="tpu_custom_call" | custom-call | tf_op jit(solution)/shard_map/advance_first/pallas_call | solution.py:402
  101.6 20.6 %all_to_all.70.received = f32[32,24,128]{2,1,0:T(8,128)S(1)} all-to-all(f32[32,24,128]{2,1,0:T(8,128)S(1)} %get-tuple-element.63), channel_id=1, replica_groups=mesh['row'=4,'col'=8] {'row','col'}, dimensions={0} | all-to-all | bytes 786432 | tf_op jit(solution)/shard_map/all_to_all | solution.py:491
  122.2 0.1 route.5
  122.2 10.0 %all_to_all.71.refs_2_ = f32[32,8,128]{2,1,0:T(8,128)S(1)} all-to-all(f32[32,8,128]{2,1,0:T(8,128)S(1)} %get-tuple-element.64), channel_id=1, replica_groups=mesh['row'=4,'col'=8] {'row','col'}, dimensions={0} | all-to-all | bytes 262144 | tf_op jit(solution)/shard_map/all_to_all | solution.py:491
  132.2 12.7 %advance_mid.4 = (f32[64,2048]{1,0:T(8,128)S(1)}, f32[128,256]{1,0:T(8,128)S(1)}, f32[32,128]{1,0:T(8,128)S(1)}, f32[32,24,128]{2,1,0:T(8,128)S(1)}, f32[64,2048...) custom-call(s32[16,4]{1,0:T(8,128)S(1)} %copy.17.refs_0_, f32[2]{0:T(128)S(1)} %copy-done.12, ...), custom_call_target="tpu_custom_call" | custom-call | tf_op jit(solution)/shard_map/advance_mid/pallas_call | solution.py:402
  144.9 15.8 %all_to_all.72.received = f32[32,24,128]{2,1,0:T(8,128)S(1)} all-to-all(f32[32,24,128]{2,1,0:T(8,128)S(1)} %get-tuple-element.69), channel_id=1, replica_groups=mesh['row'=4,'col'=8] {'row','col'}, dimensions={0} | all-to-all | bytes 786432 | tf_op jit(solution)/shard_map/all_to_all | solution.py:491
  160.7 0.1 route.6
  160.8 10.0 %all_to_all.73.refs_2_ = f32[32,8,128]{2,1,0:T(8,128)S(1)} all-to-all(f32[32,8,128]{2,1,0:T(8,128)S(1)} %get-tuple-element.70), channel_id=1, replica_groups=mesh['row'=4,'col'=8] {'row','col'}, dimensions={0} | all-to-all | bytes 262144 | tf_op jit(solution)/shard_map/all_to_all | solution.py:491
  170.8 12.7 %advance_mid.5 = (f32[64,2048]{1,0:T(8,128)S(1)}, f32[128,256]{1,0:T(8,128)S(1)}, f32[32,128]{1,0:T(8,128)S(1)}, f32[32,24,128]{2,1,0:T(8,128)S(1)}, f32[64,2048...) custom-call(s32[16,4]{1,0:T(8,128)S(1)} %copy.17.refs_0_, f32[2]{0:T(128)S(1)} %copy-done.12, ...), custom_call_target="tpu_custom_call" | custom-call | tf_op jit(solution)/shard_map/advance_mid/pallas_call | solution.py:402
  183.5 15.8 %all_to_all.74.received = f32[32,24,128]{2,1,0:T(8,128)S(1)} all-to-all(f32[32,24,128]{2,1,0:T(8,128)S(1)} %get-tuple-element.77), channel_id=1, replica_groups=mesh['row'=4,'col'=8] {'row','col'}, dimensions={0} | all-to-all | bytes 786432 | tf_op jit(solution)/shard_map/all_to_all | solution.py:491
  199.3 0.1 route.7
  199.3 10.1 %all_to_all.75.refs_2_ = f32[32,8,128]{2,1,0:T(8,128)S(1)} all-to-all(f32[32,8,128]{2,1,0:T(8,128)S(1)} %get-tuple-element.78), channel_id=1, replica_groups=mesh['row'=4,'col'=8] {'row','col'}, dimensions={0} | all-to-all | bytes 262144 | tf_op jit(solution)/shard_map/all_to_all | solution.py:491
  209.4 12.6 %advance_mid.6 = (f32[64,2048]{1,0:T(8,128)S(1)}, f32[128,256]{1,0:T(8,128)S(1)}, f32[32,128]{1,0:T(8,128)S(1)}, f32[32,24,128]{2,1,0:T(8,128)S(1)}, f32[64,2048...) custom-call(s32[16,4]{1,0:T(8,128)S(1)} %copy.17.refs_0_, f32[2]{0:T(128)S(1)} %copy-done.12, ...), custom_call_target="tpu_custom_call" | custom-call | tf_op jit(solution)/shard_map/advance_mid/pallas_call | solution.py:402
  222.0 15.8 %all_to_all.76.received = f32[32,24,128]{2,1,0:T(8,128)S(1)} all-to-all(f32[32,24,128]{2,1,0:T(8,128)S(1)} %get-tuple-element.85), channel_id=1, replica_groups=mesh['row'=4,'col'=8] {'row','col'}, dimensions={0} | all-to-all | bytes 786432 | tf_op jit(solution)/shard_map/all_to_all | solution.py:491
  237.9 0.1 route.8
  237.9 10.1 %all_to_all.77.refs_2_ = f32[32,8,128]{2,1,0:T(8,128)S(1)} all-to-all(f32[32,8,128]{2,1,0:T(8,128)S(1)} %get-tuple-element.86), channel_id=1, replica_groups=mesh['row'=4,'col'=8] {'row','col'}, dimensions={0} | all-to-all | bytes 262144 | tf_op jit(solution)/shard_map/all_to_all | solution.py:491
  248.0 13.4 %advance_mid.7 = (f32[64,2048]{1,0:T(8,128)S(1)}, f32[128,256]{1,0:T(8,128)S(1)}, f32[32,128]{1,0:T(8,128)S(1)}, f32[32,24,128]{2,1,0:T(8,128)}, f32[64,2048]{1,...) custom-call(s32[16,4]{1,0:T(8,128)S(1)} %copy.17.refs_0_, f32[2]{0:T(128)S(1)} %copy-done.12, ...), custom_call_target="tpu_custom_call" | custom-call | tf_op jit(solution)/shard_map/advance_mid/pallas_call | solution.py:402
  261.4 2.6 all-to-all-start.10
  264.0 0.6 bitcast_dynamic-update-slice_fusion.5
  264.7 12.9 %all-to-all-done.10.received = f32[32,24,128]{2,1,0:T(8,128)S(1)} async-done(((f32[32,24,128]{2,1,0:T(8,128)}), f32[32,24,128]{2,1,0:T(8,128)S(1)}, u32[]{:S(2)}, u32[]{:S(2)}) %all-to-all-start.10) | async-done | bytes 393248 | tf_op jit(solution)/shard_map/all_to_all | solution.py:491
  277.6 0.7 route.9
  278.3 3.1 all-to-all-start.11
  281.4 0.7 bitcast_dynamic-update-slice_fusion.4
  282.0 0.6 bitcast_dynamic-update-slice_fusion.3
  282.7 6.4 %all-to-all-done.11.refs_2_ = f32[32,8,128]{2,1,0:T(8,128)S(1)} async-done(((f32[32,8,128]{2,1,0:T(8,128)}), f32[32,8,128]{2,1,0:T(8,128)S(1)}, u32[]{:S(2)}, u32[]{:S(2)}) %all-to-all-start.11) | async-done | bytes 131104 | tf_op jit(solution)/shard_map/all_to_all | solution.py:491
  289.1 2.2 copy-done.3
  291.3 2.2 copy-done.7
  293.5 11.5 %advance_last.1 = (f32[64,2048]{1,0:T(8,128)S(1)}, f32[128,128]{1,0:T(8,128)}, f32[64,2048]{1,0:T(8,128)S(1)}, f32[64,128]{1,0:T(8,128)S(1)}, f32[3,64,64]{2,1,0:T(8,128)S(1)}) custom-call(s32[16,4]{1,0:T(8,128)S(1)} %copy.17.refs_0_, f32[2]{0:T(128)S(1)} %copy-done.12, f32[32,8,128]{2,1,0:T(8,128)S(1)} %all-to-all-done.11.refs_2_, ...), custom_call_target="tpu_custom_call" | custom-call | tf_op jit(solution)/shard_map/advance_last/pallas_call | solution.py:402
  305.0 0.0 copy-start.10
  305.0 0.8 copy-done.10
  305.8 2.5 all-to-all-start.12
  308.3 0.7 bitcast_dynamic-update-slice_fusion.2
  309.0 6.6 %all-to-all-done.12 = f32[32,4,128]{2,1,0:T(4,128)S(1)} async-done(((f32[32,4,128]{2,1,0:T(4,128)}), f32[32,4,128]{2,1,0:T(4,128)S(1)}, u32[]{:S(2)}, u32[]{:S(2)}) %all-to-all-start.12) | async-done | bytes 65568 | tf_op jit(solution)/shard_map/all_to_all | solution.py:491
  315.7 0.6 broadcast_in_dim.26
  316.3 2.5 all-to-all-start.13
  318.9 0.7 bitcast_dynamic-update-slice_fusion.1
  319.5 6.6 %all-to-all-done.13 = f32[32,4,128]{2,1,0:T(4,128)S(1)} async-done(((f32[32,4,128]{2,1,0:T(4,128)}), f32[32,4,128]{2,1,0:T(4,128)S(1)}, u32[]{:S(2)}, u32[]{:S(2)}) %all-to-all-start.13) | async-done | bytes 65568 | tf_op jit(solution)/shard_map/all_to_all | solution.py:491
  326.1 1.0 copy-done.11
  327.2 7.5 %finish.1 = (f32[64,2048]{1,0:T(8,128)}, f32[3,64,64]{2,1,0:T(8,128)S(1)}) custom-call(f32[128,128]{1,0:T(8,128)S(1)} %bitcast.28, f32[64,128]{1,0:T(8,128)S(1)} %get-tuple-element.102.inner, f32[64,2048]{1,0:T(8,128)S(1)} %get-tuple-element.103.applied, f32[64,2048]{1,0:T(8,128)S(1)} %copy-done.11, f32[64,2048]{1,0:T(8,128)S(1)} %get-tuple-element.100.refs_8_.previous), custom_call_target="tpu_custom_call" | custom-call | tf_op jit(solution)/shard_map/finish/pallas_call | solution.py:464
  334.7 0.7 bitcast_dynamic-update-slice_fusion
  (20 shorter events, 0.1 us)
Async XLA Ops:
  0.6 58.9 %copy-start.8 = (f32[64,2048]{1,0:T(8,128)S(1)}, f32[64,2048]{1,0:T(8,128)}, u32[]{:S(2)}) copy-start(f32[64,2048]{1,0:T(8,128)} %refs_9_.1) | copy-start | bytes 1572868
  0.6 58.9 %copy-start.13 = (s32[1024]{0:T(1024)S(1)}, s32[1024]{0:T(1024)}, u32[]{:S(2)}) copy-start(s32[1024]{0:T(1024)} %param.12) | copy-start | bytes 12292
  3.9 69.1 %copy-start.12 = (f32[2]{0:T(128)S(1)}, f32[2]{0:T(128)}, u32[]{:S(2)}) copy-start(f32[2]{0:T(128)} %refs_1_.11) | copy-start | bytes 28
  3.9 69.1 %copy-start.14 = (s32[128]{0:T(128)S(1)}, s32[128]{0:T(128)}, u32[]{:S(2)}) copy-start(s32[128]{0:T(128)} %param.11) | copy-start | bytes 1540
  3.9 55.6 %all-to-all-start = ((bf16[8,128,1024]{2,1,0:T(8,128)(2,1)}), bf16[8,128,1024]{2,1,0:T(8,128)(2,1)S(1)}, u32[]{:S(2)}, u32[]{:S(2)}) async-start(bf16[8,128,1024]{2,1,0:T(8,128)(2,1)} %bitcast.31), calls=%async_computation | async-start | bytes 4194304 | tf_op jit(solution)/shard_map/all_to_all | solution.py:504
  67.2 2.0 copy-start
  69.2 17.5 %copy-start.15 = (s32[16,4]{0,1:T(4,128)S(1)}, s32[16,4]{0,1:T(4,128)}, u32[]{:S(2)}) copy-start(s32[16,4]{0,1:T(4,128)} %param.10) | copy-start | bytes 772
  69.2 22.0 %all-to-all-start.1 = ((f32[32,16,128]{2,1,0:T(8,128)}), f32[32,16,128]{2,1,0:T(8,128)S(1)}, u32[]{:S(2)}, u32[]{:S(2)}) async-start(f32[32,16,128]{2,1,0:T(8,128)} %bitcast.3), calls=%async_computation.1 | async-start | bytes 524288 | tf_op jit(solution)/shard_map/all_to_all | solution.py:491
  73.0 2.8 copy-start.9
  79.8 2.0 copy-start.4
  81.7 5.2 %collective-permute-start = (f32[64,128]{1,0:T(8,128)S(1)}, f32[64,128]{1,0:T(8,128)S(1)}, u32[]{:S(2)}, u32[]{:S(2)}) collective-permute-start(f32[64,128]{1,0:T(8,128)S(1)} %get-tuple-element.58), channel_id=1, source_target_pairs={{0,1},{1,2},{2,3},{3,4},{4,5},{5,6},{6,7},{7,8},{8,9},{9,10},{10,1... | collective-permute-start | bytes 98312 | tf_op jit(solution)/shard_map/ppermute | solution.py:496
  85.4 5.8 %collective-permute-start.1 = (f32[64,128]{1,0:T(8,128)S(1)}, f32[64,128]{1,0:T(8,128)S(1)}, u32[]{:S(2)}, u32[]{:S(2)}) collective-permute-start(f32[64,128]{1,0:T(8,128)S(1)} %get-tuple-element.58), channel_id=1, source_target_pairs={{1,0},{2,1},{3,2},{4,3},{5,4},{6,5},{7,6},{8,7},{9,8},{10,9},{11,1... | collective-permute-start | bytes 98312 | tf_op jit(solution)/shard_map/ppermute | solution.py:496
  91.2 2.2 copy-start.1
  93.4 2.2 copy-start.5
  95.6 36.6 %copy-start.2 = (bf16[1024,2048]{1,0:T(8,128)(2,1)S(1)}, bf16[1024,2048]{1,0:T(8,128)(2,1)}, u32[]{:S(2)}) copy-start(bf16[1024,2048]{1,0:T(8,128)(2,1)} %copy-done) | copy-start | bytes 12582916
  170.8 38.6 %copy-start.6 = (bf16[16,512,256]{2,1,0:T(8,128)(2,1)S(1)}, bf16[16,512,256]{2,1,0:T(8,128)(2,1)}, u32[]{:S(2)}) copy-start(bf16[16,512,256]{2,1,0:T(8,128)(2,1)} %copy-done.4) | copy-start | bytes 12582916
  261.4 16.2 %all-to-all-start.10 = ((f32[32,24,128]{2,1,0:T(8,128)}), f32[32,24,128]{2,1,0:T(8,128)S(1)}, u32[]{:S(2)}, u32[]{:S(2)}) async-start(f32[32,24,128]{2,1,0:T(8,128)} %get-tuple-element.93), calls=%async_computation.10 | async-start | bytes 786432 | tf_op jit(solution)/shard_map/all_to_all | solution.py:491
  278.3 10.8 %all-to-all-start.11 = ((f32[32,8,128]{2,1,0:T(8,128)}), f32[32,8,128]{2,1,0:T(8,128)S(1)}, u32[]{:S(2)}, u32[]{:S(2)}) async-start(f32[32,8,128]{2,1,0:T(8,128)} %get-tuple-element.94), calls=%async_computation.11 | async-start | bytes 262144 | tf_op jit(solution)/shard_map/all_to_all | solution.py:491
  289.1 2.2 copy-start.3
  291.3 2.2 copy-start.7
  305.0 0.8 copy-start.10
  305.8 9.8 %all-to-all-start.12 = ((f32[32,4,128]{2,1,0:T(4,128)}), f32[32,4,128]{2,1,0:T(4,128)S(1)}, u32[]{:S(2)}, u32[]{:S(2)}) async-start(f32[32,4,128]{2,1,0:T(4,128)} %bitcast.6), calls=%async_computation.12 | async-start | bytes 131072 | tf_op jit(solution)/shard_map/all_to_all | solution.py:491
  316.3 9.8 %all-to-all-start.13 = ((f32[32,4,128]{2,1,0:T(4,128)}), f32[32,4,128]{2,1,0:T(4,128)S(1)}, u32[]{:S(2)}, u32[]{:S(2)}) async-start(f32[32,4,128]{2,1,0:T(4,128)} %broadcast_in_dim.26), calls=%async_computation.13 | async-start | bytes 131072 | tf_op jit(solution)/shard_map/all_to_all | solution.py:491
  326.1 1.0 copy-start.11
